TPU v7x, 256 devices: a whole 4x4x8 slice. The times are simulated.
256 devices in a mesh: reg: 8 (over y, core), prod: 32 (over x, z).
Axes of the slice: x: 4, y: 4, z: 8, core: 2. Of those that a mesh axis runs over, the one named last changes fastest.
Arguments:
- bottom_series_predictions: float32 [256, 1024, 128], P('reg', 'prod'), may hold values from -6 to 6
- group_item_predictions: float32 [32, 1024, 128], P('reg', 'prod'), may hold values from -18 to 18
- area_class_predictions: float32 [256, 32, 128], P('reg', 'prod'), may hold values from -18 to 18
- group_class_predictions: float32 [32, 32, 128], P('reg'), may hold values from -48 to 48
- bottom_series_precision: float32 [256, 1024], P('reg', 'prod'), may hold values from 0.5 to 5
- group_item_precision: float32 [32, 1024], P('reg', 'prod'), may hold values from 0.02 to 0.5
- area_class_precision: float32 [256, 32], P('reg', 'prod'), may hold values from 0.02 to 0.5
- group_class_precision: float32 [32, 32], P('reg'), may hold values from 0.002 to 0.05
- group_area_partition: int32 [32, 128], replicated, may hold values from -1 to 255, as said below
- class_item_partition: int32 [32, 128], replicated, may hold values from -1 to 1023, as said below
Outputs:
- solution_field: float32 [256, 1024, 128], P('reg', 'prod')
- residual: float32 [256, 1024, 128], P('reg', 'prod')
Inputs may be any that keep to these rules, and one draw needn't show every extreme that they name: `group_area_partition`: every region stands in exactly one row; each row holds its parent's regions in its first slots and -1 in the rest; a parent has 1 to 128 regions, and some parent has exactly 128. `class_item_partition`: every product stands in exactly one row; each row holds its category's products in its first slots and -1 in the rest; a category has 1 to 128 products, and some category has exactly 128.
All inputs are finite; a program needn't handle non-finite values.
Results may differ from a plain program's by a relative error of at most 0.00011.
Values sent between devices are 32-bit elements; how exact they have to be, the bound alone decides.
No kernel may reach another device: no remote copies, remote signals or barrier semaphores. Data moves between devices by JAX's collectives and lax.ppermute only.
A program may use at most 64 MiB of HBM per device.

v0:
```python
import jax
import jax.numpy as jnp
from jax import lax
from jax.sharding import Mesh
from jax.sharding import PartitionSpec as P

ITERATIONS = 2
REG = ("reg_0", "reg_1")
PROD = ("prod_0", "prod_1")


def copy_for_each(value, axis):
    copies = jnp.broadcast_to(value, (lax.axis_size(axis), *value.shape))
    return lax.all_to_all(copies, axis, split_axis=0, concat_axis=0, tiled=True)


def joined_along(pieces, dim):
    shape = list(pieces.shape[1:])
    shape[dim] *= pieces.shape[0]
    return jnp.moveaxis(pieces, 0, dim).reshape(shape)


def gathered_copies(value, axis, dim):
    pieces = copy_for_each(value, axis)
    return joined_along(pieces, dim)


def split_up(value, dim, length):
    before, after = (value.shape[:dim], value.shape[dim + 1 :])
    return jnp.moveaxis(value.reshape(*before, length, -1, *after), dim, 0)


def sent_and_summed(value, axis, dim):
    length = lax.axis_size(axis)
    pieces = lax.all_to_all(split_up(value, dim, length), axis, 0, 0, tiled=True)
    return jnp.sum(pieces, axis=0)


def rows_for(lines, length):
    spare = -len(lines) % length
    return jnp.pad(lines, [(0, spare)] + [(0, 0)] * (lines.ndim - 1))


def sum_by_parts(value, axes):
    lines = value.reshape(-1, value.shape[-1])
    padded = rows_for(lines, lax.axis_size(axes))
    whole = gathered_copies(sent_and_summed(padded, axes, 0), axes, 0)
    return lax.slice_in_dim(whole, 0, len(lines)).reshape(value.shape)


def taken_together(value, axis):
    return copy_for_each(value, axis).sum(axis=0)


def one_axis_at_a_time(value, axes):
    far, near = axes
    return taken_together(taken_together(value, near), far)


def in_one(arrays, axis):
    vector, at, finished = (jnp.concatenate([a.reshape(-1) for a in arrays]), 0, [])
    so_far = one_axis_at_a_time(vector, axis)
    for a in arrays:
        finished.append(so_far[at : at + a.size].reshape(a.shape))
        at += a.size
    return tuple(finished)


def member_local(table, first, count):
    items = first + jnp.arange(count, dtype=jnp.int32)
    return jnp.any(table[:, :, None] == items[None, None, :], axis=1).astype(jnp.float32)


def on_device(
    bottom_series_predictions,
    group_item_predictions,
    area_class_predictions,
    group_class_predictions,
    bottom_series_precision,
    group_item_precision,
    area_class_precision,
    group_class_precision,
    group_area_partition,
    class_item_partition,
):
    high = lax.Precision.HIGHEST
    areas_overall, items_overall, horizon_length = bottom_series_predictions.shape
    area_index_table = member_local(
        group_area_partition, lax.axis_index(REG) * areas_overall, areas_overall
    )
    item_index_table = member_local(
        class_item_partition, lax.axis_index(PROD) * items_overall, items_overall
    )

    def disaggregate_onto(upper, lower):
        block = area_index_table
        total = jnp.einsum("pr,pqh->rqh", block, gathered_copies(upper, REG, 0), precision=high)
        block = item_index_table
        return total + jnp.einsum(
            "crh,cq->rqh", gathered_copies(lower, PROD, 0), block, precision=high
        )

    def replicate_across(corner):
        return jnp.einsum("pch,cq->pqh", corner, item_index_table, precision=high)

    def operate(field):
        rows_local = jnp.einsum("pr,rqh->pqh", area_index_table, field, precision=high)
        row_share = sent_and_summed(rows_local, REG, 0)
        col_share = sent_and_summed(
            jnp.einsum("cq,rqh->crh", item_index_table, field, precision=high), PROD, 0
        )
        partial_corner = jnp.einsum("pqh,cq->pch", row_share, item_index_table, precision=high)
        corner_share = sum_by_parts(partial_corner, PROD)
        upper = group_item_precision[:, :, None] * row_share + replicate_across(
            group_class_precision[:, :, None] * corner_share
        )
        lower = jnp.transpose(area_class_precision)[:, :, None] * col_share
        return bottom_series_precision[:, :, None] * field + disaggregate_onto(upper, lower)

    major_axis_first = group_item_precision[:, :, None] * group_item_predictions + replicate_across(
        group_class_precision[:, :, None] * group_class_predictions
    )
    lower_leading = jnp.transpose(
        area_class_precision[:, :, None] * area_class_predictions, (1, 0, 2)
    )
    system_source_term = bottom_series_precision[
        :, :, None
    ] * bottom_series_predictions + disaggregate_onto(major_axis_first, lower_leading)

    def two_products(vector, image):
        return in_one(
            (jnp.sum(vector * vector), jnp.sum(vector * image)),
            (("reg_0", "reg_1"), ("prod_0", "prod_1")),
        )

    solution_field = jnp.zeros_like(system_source_term)
    residual = system_source_term
    image = operate(residual)
    norm_now, product = two_products(residual, image)
    alpha = norm_now / product
    direction, along = (residual, image)
    for step in range(ITERATIONS):
        solution_field = solution_field + alpha * direction
        residual = residual - alpha * along
        if step + 1 < ITERATIONS:
            image = operate(residual)
            norm_next, product = two_products(residual, image)
            ratio = norm_next / norm_now
            alpha = norm_next / (product - ratio * norm_next / alpha)
            direction = residual + ratio * direction
            along = image + ratio * along
            norm_now = norm_next
    return (solution_field, residual)


def solution(mesh):
    finer = Mesh(mesh.devices.reshape(4, 2, 4, 8), ("reg_0", "reg_1", "prod_0", "prod_1"))
    return jax.shard_map(
        on_device,
        mesh=finer,
        in_specs=(
            P(REG, PROD, None),
            P(REG, PROD, None),
            P(REG, PROD, None),
            P(REG, None, None),
            P(REG, PROD),
            P(REG, PROD),
            P(REG, PROD),
            P(REG, None),
            P(),
            P(),
        ),
        out_specs=(P(REG, PROD, None), P(REG, PROD, None)),
        check_vma=False,
    )
```

profile of v0, /device:TPU:1, one launch (start us, length us, event | category | flops | bytes accessed | tf_op | source)
XLA Modules:
  0.0 309.2 jit_solution(5893511679883991110)
XLA Ops:
  4.1 6.8 %all-to-all-start = ((f32[8,4,32,128]{3,1,2,0:T(4,128)}), f32[8,4,32,128]{3,1,2,0:T(4,128)S(1)}, u32[]{:S(2)}, u32[]{:S(2)}) async-start(f32[8,4,32,128]{3,1,2,0:T(4,128)} %broadcast_in_dim.24), calls=%async_computation | async-start | bytes 1048576 | tf_op jit(solution)/shard_map/all_to_all | solution.py:14
  11.6 8.7 %all-to-all-done = f32[8,4,32,128]{3,1,2,0:T(4,128)S(1)} async-done(((f32[8,4,32,128]{3,1,2,0:T(4,128)}), f32[8,4,32,128]{3,1,2,0:T(4,128)S(1)}, u32[]{:S(2)}, u32[]{:S(2)}) %all-to-all-start) | async-done | bytes 524320 | tf_op jit(solution)/shard_map/all_to_all | solution.py:14
  21.2 10.3 %all-to-all-start.1 = ((f32[32,1,32,128]{3,2,1,0:T(8,128)}), f32[32,1,32,128]{3,2,1,0:T(8,128)S(1)}, u32[]{:S(2)}, u32[]{:S(2)}) async-start(f32[32,1,32,128]{3,2,1,0:T(8,128)} %broadcast_in_dim.25), calls=%async_computation.1 | async-start | bytes 1048576 | tf_op jit(solution)/shard_map/all_to_all | solution.py:14
  33.9 11.8 %all-to-all-done.1 = f32[32,1,32,128]{3,2,1,0:T(8,128)S(1)} async-done(((f32[32,1,32,128]{3,2,1,0:T(8,128)}), f32[32,1,32,128]{3,2,1,0:T(8,128)S(1)}, u32[]{:S(2)}, u32[]{:S(2)}) %all-to-all-start.1) | async-done | bytes 524320 | tf_op jit(solution)/shard_map/all_to_all | solution.py:14
  47.8 15.8 %all_to_all.94 = f32[8,4,32,128]{3,2,1,0:T(8,128)S(1)} all-to-all(f32[8,4,32,128]{3,2,1,0:T(8,128)S(1)} %copy.125), channel_id=1, replica_groups=mesh['reg_0'=4,'reg_1'=2,'prod_0'=4,'prod_1'=8] {'reg_0','reg_1'}, dimensions={0} | all-to-all | bytes 1048576 | tf_op jit(solution)/shard_map/all_to_all | solution.py:35
  63.8 13.8 %all_to_all.95 = f32[32,4,128]{2,1,0:T(4,128)S(1)} all-to-all(f32[32,4,128]{2,1,0:T(4,128)S(1)} %bitcast.122), channel_id=1, replica_groups=mesh['reg_0'=4,'reg_1'=2,'prod_0'=4,'prod_1'=8] {'prod_0','prod_1'}, dimensions={0} | all-to-all | bytes 131072 | tf_op jit(solution)/shard_map/all_to_all | solution.py:35
  78.2 3.9 %all-to-all-start.4 = ((f32[32,4,128]{2,1,0:T(4,128)}), f32[32,4,128]{2,1,0:T(4,128)S(1)}, u32[]{:S(2)}, u32[]{:S(2)}) async-start(f32[32,4,128]{2,1,0:T(4,128)} %broadcast_in_dim.52), calls=%async_computation.4 | async-start | bytes 131072 | tf_op jit(solution)/shard_map/all_to_all | solution.py:14
  83.9 7.0 %all-to-all-done.4 = f32[32,4,128]{2,1,0:T(4,128)S(1)} async-done(((f32[32,4,128]{2,1,0:T(4,128)}), f32[32,4,128]{2,1,0:T(4,128)S(1)}, u32[]{:S(2)}, u32[]{:S(2)}) %all-to-all-start.4) | async-done | bytes 65568 | tf_op jit(solution)/shard_map/all_to_all | solution.py:14
  91.0 3.9 %all-to-all-start.6 = ((f32[32,1,32,128]{3,2,1,0:T(8,128)}), f32[32,1,32,128]{3,2,1,0:T(8,128)S(1)}, u32[]{:S(2)}, u32[]{:S(2)}) async-start(f32[32,1,32,128]{3,2,1,0:T(8,128)} %copy.131), calls=%async_computation.6 | async-start | bytes 1048576 | tf_op jit(solution)/shard_map/all_to_all | solution.py:35
  95.2 11.3 %all-to-all-done.6 = f32[32,1,32,128]{3,2,1,0:T(8,128)S(1)} async-done(((f32[32,1,32,128]{3,2,1,0:T(8,128)}), f32[32,1,32,128]{3,2,1,0:T(8,128)S(1)}, u32[]{:S(2)}, u32[]{:S(2)}) %all-to-all-start.6) | async-done | bytes 524320 | tf_op jit(solution)/shard_map/all_to_all | solution.py:35
  107.4 9.4 %all-to-all-start.5 = ((f32[8,4,32,128]{3,1,2,0:T(4,128)}), f32[8,4,32,128]{3,1,2,0:T(4,128)S(1)}, u32[]{:S(2)}, u32[]{:S(2)}) async-start(f32[8,4,32,128]{3,1,2,0:T(4,128)} %broadcast_in_dim.53), calls=%async_computation.5 | async-start | bytes 1048576 | tf_op jit(solution)/shard_map/all_to_all | solution.py:14
  116.9 9.4 %all-to-all-done.5 = f32[8,4,32,128]{3,1,2,0:T(4,128)S(1)} async-done(((f32[8,4,32,128]{3,1,2,0:T(4,128)}), f32[8,4,32,128]{3,1,2,0:T(4,128)S(1)}, u32[]{:S(2)}, u32[]{:S(2)}) %all-to-all-start.5) | async-done | bytes 524320 | tf_op jit(solution)/shard_map/all_to_all | solution.py:14
  127.2 5.5 %all-to-all-start.7 = ((f32[32,1,32,128]{3,2,1,0:T(8,128)}), f32[32,1,32,128]{3,2,1,0:T(8,128)S(1)}, u32[]{:S(2)}, u32[]{:S(2)}) async-start(f32[32,1,32,128]{3,2,1,0:T(8,128)} %broadcast_in_dim.54), calls=%async_computation.7 | async-start | bytes 1048576 | tf_op jit(solution)/shard_map/all_to_all | solution.py:14
  132.8 13.9 %all-to-all-done.7 = f32[32,1,32,128]{3,2,1,0:T(8,128)S(1)} async-done(((f32[32,1,32,128]{3,2,1,0:T(8,128)}), f32[32,1,32,128]{3,2,1,0:T(8,128)S(1)}, u32[]{:S(2)}, u32[]{:S(2)}) %all-to-all-start.7) | async-done | bytes 524320 | tf_op jit(solution)/shard_map/all_to_all | solution.py:14
  147.4 1.3 multiply_reduce_fusion.3
  148.7 1.4 pad_maximum_fusion
  150.1 16.2 %all_to_all.96 = f32[32,1,2]{2,1,0:T(1,128)S(1)} all-to-all(f32[32,1,2]{2,1,0:T(1,128)S(1)} %broadcast_in_dim.55), channel_id=1, replica_groups=mesh['reg_0'=4,'reg_1'=2,'prod_0'=4,'prod_1'=8] {'prod_0','prod_1'}, dimensions={0} | all-to-all | bytes 512 | tf_op jit(solution)/shard_map/all_to_all | solution.py:14
  166.4 9.7 %all_to_all.97 = f32[8,1,2]{2,1,0:T(1,128)S(1)} all-to-all(f32[8,1,2]{2,1,0:T(1,128)S(1)} %broadcast_in_dim.56), channel_id=1, replica_groups=mesh['reg_0'=4,'reg_1'=2,'prod_0'=4,'prod_1'=8] {'reg_0','reg_1'}, dimensions={0} | all-to-all | bytes 128 | tf_op jit(solution)/shard_map/all_to_all | solution.py:14
  178.7 12.5 %all_to_all.98 = f32[8,4,32,128]{3,2,1,0:T(8,128)S(1)} all-to-all(f32[8,4,32,128]{3,2,1,0:T(8,128)S(1)} %copy.138), channel_id=1, replica_groups=mesh['reg_0'=4,'reg_1'=2,'prod_0'=4,'prod_1'=8] {'reg_0','reg_1'}, dimensions={0} | all-to-all | bytes 1048576 | tf_op jit(solution)/shard_map/all_to_all | solution.py:35
  191.3 11.8 %all_to_all.99 = f32[32,4,128]{2,1,0:T(4,128)S(1)} all-to-all(f32[32,4,128]{2,1,0:T(4,128)S(1)} %bitcast.123), channel_id=1, replica_groups=mesh['reg_0'=4,'reg_1'=2,'prod_0'=4,'prod_1'=8] {'prod_0','prod_1'}, dimensions={0} | all-to-all | bytes 131072 | tf_op jit(solution)/shard_map/all_to_all | solution.py:35
  203.8 4.0 %all-to-all-start.12 = ((f32[32,4,128]{2,1,0:T(4,128)}), f32[32,4,128]{2,1,0:T(4,128)S(1)}, u32[]{:S(2)}, u32[]{:S(2)}) async-start(f32[32,4,128]{2,1,0:T(4,128)} %broadcast_in_dim.57), calls=%async_computation.12 | async-start | bytes 131072 | tf_op jit(solution)/shard_map/all_to_all | solution.py:14
  209.7 6.9 %all-to-all-done.12 = f32[32,4,128]{2,1,0:T(4,128)S(1)} async-done(((f32[32,4,128]{2,1,0:T(4,128)}), f32[32,4,128]{2,1,0:T(4,128)S(1)}, u32[]{:S(2)}, u32[]{:S(2)}) %all-to-all-start.12) | async-done | bytes 65568 | tf_op jit(solution)/shard_map/all_to_all | solution.py:14
  216.6 3.9 %all-to-all-start.14 = ((f32[32,1,32,128]{3,2,1,0:T(8,128)}), f32[32,1,32,128]{3,2,1,0:T(8,128)S(1)}, u32[]{:S(2)}, u32[]{:S(2)}) async-start(f32[32,1,32,128]{3,2,1,0:T(8,128)} %copy.144), calls=%async_computation.14 | async-start | bytes 1048576 | tf_op jit(solution)/shard_map/all_to_all | solution.py:35
  220.9 11.5 %all-to-all-done.14 = f32[32,1,32,128]{3,2,1,0:T(8,128)S(1)} async-done(((f32[32,1,32,128]{3,2,1,0:T(8,128)}), f32[32,1,32,128]{3,2,1,0:T(8,128)S(1)}, u32[]{:S(2)}, u32[]{:S(2)}) %all-to-all-start.14) | async-done | bytes 524320 | tf_op jit(solution)/shard_map/all_to_all | solution.py:35
  233.2 9.3 %all-to-all-start.13 = ((f32[8,4,32,128]{3,1,2,0:T(4,128)}), f32[8,4,32,128]{3,1,2,0:T(4,128)S(1)}, u32[]{:S(2)}, u32[]{:S(2)}) async-start(f32[8,4,32,128]{3,1,2,0:T(4,128)} %broadcast_in_dim.58), calls=%async_computation.13 | async-start | bytes 1048576 | tf_op jit(solution)/shard_map/all_to_all | solution.py:14
  242.6 9.4 %all-to-all-done.13 = f32[8,4,32,128]{3,1,2,0:T(4,128)S(1)} async-done(((f32[8,4,32,128]{3,1,2,0:T(4,128)}), f32[8,4,32,128]{3,1,2,0:T(4,128)S(1)}, u32[]{:S(2)}, u32[]{:S(2)}) %all-to-all-start.13) | async-done | bytes 524320 | tf_op jit(solution)/shard_map/all_to_all | solution.py:14
  252.8 5.5 %all-to-all-start.15 = ((f32[32,1,32,128]{3,2,1,0:T(8,128)}), f32[32,1,32,128]{3,2,1,0:T(8,128)S(1)}, u32[]{:S(2)}, u32[]{:S(2)}) async-start(f32[32,1,32,128]{3,2,1,0:T(8,128)} %broadcast_in_dim.59), calls=%async_computation.15 | async-start | bytes 1048576 | tf_op jit(solution)/shard_map/all_to_all | solution.py:14
  258.4 13.9 %all-to-all-done.15 = f32[32,1,32,128]{3,2,1,0:T(8,128)S(1)} async-done(((f32[32,1,32,128]{3,2,1,0:T(8,128)}), f32[32,1,32,128]{3,2,1,0:T(8,128)S(1)}, u32[]{:S(2)}, u32[]{:S(2)}) %all-to-all-start.15) | async-done | bytes 524320 | tf_op jit(solution)/shard_map/all_to_all | solution.py:14
  273.0 1.3 multiply_reduce_fusion.1
  274.3 1.4 pad_maximum_fusion.1
  275.7 16.2 %all_to_all.100 = f32[32,1,2]{2,1,0:T(1,128)S(1)} all-to-all(f32[32,1,2]{2,1,0:T(1,128)S(1)} %broadcast_in_dim.60), channel_id=1, replica_groups=mesh['reg_0'=4,'reg_1'=2,'prod_0'=4,'prod_1'=8] {'prod_0','prod_1'}, dimensions={0} | all-to-all | bytes 512 | tf_op jit(solution)/shard_map/all_to_all | solution.py:14
  292.0 9.7 %all_to_all.101 = f32[8,1,2]{2,1,0:T(1,128)S(1)} all-to-all(f32[8,1,2]{2,1,0:T(1,128)S(1)} %broadcast_in_dim.61), channel_id=1, replica_groups=mesh['reg_0'=4,'reg_1'=2,'prod_0'=4,'prod_1'=8] {'reg_0','reg_1'}, dimensions={0} | all-to-all | bytes 128 | tf_op jit(solution)/shard_map/all_to_all | solution.py:14
  (77 shorter events, 25.3 us)
Async XLA Ops:
  0.6 0.7 copy-start.3
  1.3 0.7 copy-start.1
  1.4 0.7 copy-start.2
  4.1 6.8 %copy-start.4 = (f32[32,1,128]{2,1,0:T(1,128)S(1)}, f32[32,1,128]{2,1,0:T(1,128)}, u32[]{:S(2)}) copy-start(f32[32,1,128]{2,1,0:T(1,128)} %param.12) | copy-start | bytes 49156
  4.1 16.3 %all-to-all-start = ((f32[8,4,32,128]{3,1,2,0:T(4,128)}), f32[8,4,32,128]{3,1,2,0:T(4,128)S(1)}, u32[]{:S(2)}, u32[]{:S(2)}) async-start(f32[8,4,32,128]{3,1,2,0:T(4,128)} %broadcast_in_dim.24), calls=%async_computation | async-start | bytes 1048576 | tf_op jit(solution)/shard_map/all_to_all | solution.py:14
  10.9 0.7 copy-start.7
  21.2 24.4 %all-to-all-start.1 = ((f32[32,1,32,128]{3,2,1,0:T(8,128)}), f32[32,1,32,128]{3,2,1,0:T(8,128)S(1)}, u32[]{:S(2)}, u32[]{:S(2)}) async-start(f32[32,1,32,128]{3,2,1,0:T(8,128)} %broadcast_in_dim.25), calls=%async_computation.1 | async-start | bytes 1048576 | tf_op jit(solution)/shard_map/all_to_all | solution.py:14
  31.6 0.7 copy-start.5
  32.3 0.7 copy-start.6
  33.9 12.5 %copy-start = (f32[32,32,128]{2,1,0:T(8,128)S(1)}, f32[32,32,128]{2,1,0:T(8,128)}, u32[]{:S(2)}) copy-start(f32[32,32,128]{2,1,0:T(8,128)} %param.10) | copy-start | bytes 1572868
  78.2 12.7 %all-to-all-start.4 = ((f32[32,4,128]{2,1,0:T(4,128)}), f32[32,4,128]{2,1,0:T(4,128)S(1)}, u32[]{:S(2)}, u32[]{:S(2)}) async-start(f32[32,4,128]{2,1,0:T(4,128)} %broadcast_in_dim.52), calls=%async_computation.4 | async-start | bytes 131072 | tf_op jit(solution)/shard_map/all_to_all | solution.py:14
  91.0 15.6 %all-to-all-start.6 = ((f32[32,1,32,128]{3,2,1,0:T(8,128)}), f32[32,1,32,128]{3,2,1,0:T(8,128)S(1)}, u32[]{:S(2)}, u32[]{:S(2)}) async-start(f32[32,1,32,128]{3,2,1,0:T(8,128)} %copy.131), calls=%async_computation.6 | async-start | bytes 1048576 | tf_op jit(solution)/shard_map/all_to_all | solution.py:35
  107.4 18.9 %all-to-all-start.5 = ((f32[8,4,32,128]{3,1,2,0:T(4,128)}), f32[8,4,32,128]{3,1,2,0:T(4,128)S(1)}, u32[]{:S(2)}, u32[]{:S(2)}) async-start(f32[8,4,32,128]{3,1,2,0:T(4,128)} %broadcast_in_dim.53), calls=%async_computation.5 | async-start | bytes 1048576 | tf_op jit(solution)/shard_map/all_to_all | solution.py:14
  127.2 19.5 %all-to-all-start.7 = ((f32[32,1,32,128]{3,2,1,0:T(8,128)}), f32[32,1,32,128]{3,2,1,0:T(8,128)S(1)}, u32[]{:S(2)}, u32[]{:S(2)}) async-start(f32[32,1,32,128]{3,2,1,0:T(8,128)} %broadcast_in_dim.54), calls=%async_computation.7 | async-start | bytes 1048576 | tf_op jit(solution)/shard_map/all_to_all | solution.py:14
  203.8 12.7 %all-to-all-start.12 = ((f32[32,4,128]{2,1,0:T(4,128)}), f32[32,4,128]{2,1,0:T(4,128)S(1)}, u32[]{:S(2)}, u32[]{:S(2)}) async-start(f32[32,4,128]{2,1,0:T(4,128)} %broadcast_in_dim.57), calls=%async_computation.12 | async-start | bytes 131072 | tf_op jit(solution)/shard_map/all_to_all | solution.py:14
  216.6 15.7 %all-to-all-start.14 = ((f32[32,1,32,128]{3,2,1,0:T(8,128)}), f32[32,1,32,128]{3,2,1,0:T(8,128)S(1)}, u32[]{:S(2)}, u32[]{:S(2)}) async-start(f32[32,1,32,128]{3,2,1,0:T(8,128)} %copy.144), calls=%async_computation.14 | async-start | bytes 1048576 | tf_op jit(solution)/shard_map/all_to_all | solution.py:35
  233.2 18.8 %all-to-all-start.13 = ((f32[8,4,32,128]{3,1,2,0:T(4,128)}), f32[8,4,32,128]{3,1,2,0:T(4,128)S(1)}, u32[]{:S(2)}, u32[]{:S(2)}) async-start(f32[8,4,32,128]{3,1,2,0:T(4,128)} %broadcast_in_dim.58), calls=%async_computation.13 | async-start | bytes 1048576 | tf_op jit(solution)/shard_map/all_to_all | solution.py:14
  252.8 19.5 %all-to-all-start.15 = ((f32[32,1,32,128]{3,2,1,0:T(8,128)}), f32[32,1,32,128]{3,2,1,0:T(8,128)S(1)}, u32[]{:S(2)}, u32[]{:S(2)}) async-start(f32[32,1,32,128]{3,2,1,0:T(8,128)} %broadcast_in_dim.59), calls=%async_computation.15 | async-start | bytes 1048576 | tf_op jit(solution)/shard_map/all_to_all | solution.py:14
where the time goes:
time: 311 us; the launch traced here: 309 us
  blocking collectives  106 us (34%)
  waiting for transfers between devices  104 us (33%)
  starting transfers between devices  62.4 us (20%)
  local copies, waits for them, and re-layouts  15.6 us (5%)
  matrix products  9.88 us (3%)
  between operations  6.77 us (2%)
  other arithmetic  5.26 us (2%)
    all_to_all x8, waiting for transfers between devices, copy_for_each(): return lax.all_to_all(copies, axis, split_axis=0, concat_axis=0, tiled=True)  81 us
    all_to_all x8, starting transfers between devices, copy_for_each(): return lax.all_to_all(copies, axis, split_axis=0, concat_axis=0, tiled=True)  54.6 us
    all_to_all x4, blocking collectives, sent_and_summed(): lax.all_to_all(split_up(value, dim, length), axis, 0, 0, tiled=True)  53.8 us
    all_to_all x4, blocking collectives, copy_for_each(): return lax.all_to_all(copies, axis, split_axis=0, concat_axis=0, tiled=True)  51.8 us
    all_to_all x2, waiting for transfers between devices, sent_and_summed(): lax.all_to_all(split_up(value, dim, length), axis, 0, 0, tiled=True)  22.7 us
    all_to_all x2, starting transfers between devices, sent_and_summed(): lax.all_to_all(split_up(value, dim, length), axis, 0, 0, tiled=True)  7.78 us
    broadcast_in_dim x12, local copies, waits for them, and re-layouts, copy_for_each(): copies = jnp.broadcast_to(value, (lax.axis_size(axis), *value.shape))  6.46 us
  transfers between devices with their start and end apart: 10, of which 10 were waited for; matrix products, arithmetic and copies ran while one was open for 2% of the time, Pallas kernels for 0%

commit v1 on v0

v1 whole, which is shorter than its diff:
```python
import jax
import jax.numpy as jnp
from jax import lax
from jax.experimental import pallas as pl
from jax.experimental.pallas import tpu as pltpu
from jax.sharding import Mesh
from jax.sharding import PartitionSpec as P

F32 = jnp.float32
BF16 = jnp.bfloat16
REG = ("y", "core")
PROD = ("x", "z")
SPLIT = ("y", "core", "x")
GROUPS = 32
HIGH = lax.Precision.HIGHEST


def iota(shape, dim):
    return lax.broadcasted_iota(jnp.int32, shape, dim)


def parts(value):
    high = value.astype(BF16)
    rest = value - high.astype(F32)
    middle = rest.astype(BF16)
    return high, middle, (rest - middle.astype(F32)).astype(BF16)


def left_dot(flags, value):
    return sum(jnp.dot(flags, p, preferred_element_type=F32) for p in parts(value))


def right_dot(value, flags):
    return sum(jnp.dot(p, flags, preferred_element_type=F32) for p in parts(value))


def over_lanes(flags, value):
    dims = (((1,), (1,)), ((), ()))
    return sum(lax.dot_general(flags, p, dims, preferred_element_type=F32) for p in parts(value))


def over_rows(value, flags):
    dims = (((0,), (0,)), ((), ()))
    return sum(lax.dot_general(p, flags, dims, preferred_element_type=F32) for p in parts(value))


def swapped(pieces):
    group = iota(pieces[0].shape, 1) // 32
    odd, upper = (group & 1) == 1, group >= 2
    a = []
    for i in (0, 2):
        a.append(jnp.where(odd, pltpu.roll(pieces[i + 1], 32, 1), pieces[i]))
        a.append(jnp.where(odd, pieces[i + 1], pltpu.roll(pieces[i], 96, 1)))
    return (
        jnp.where(upper, pltpu.roll(a[2], 64, 1), a[0]),
        jnp.where(upper, pltpu.roll(a[3], 64, 1), a[1]),
        jnp.where(upper, a[2], pltpu.roll(a[0], 64, 1)),
        jnp.where(upper, a[3], pltpu.roll(a[1], 64, 1)),
    )


def class_flags(places):
    row = iota((64, 128), 0)
    at = (row // 8) * 4 + row % 4 == places
    second = (row & 4) == 4
    one, none = jnp.ones((64, 128), F32), jnp.zeros((64, 128), F32)
    first_flags = jnp.where(at, jnp.where(second, none, one), none)
    second_flags = jnp.where(at, jnp.where(second, one, none), none)
    return first_flags.astype(BF16), second_flags.astype(BF16)


def weighted(field, precision):
    return (field.reshape(32, 4, 8, 128) * precision.reshape(32, 1, 8, 128)).reshape(1024, 128)


def region_mix(field, precision, group_precision, flags, flags_t):
    return weighted(field, precision) + left_dot(
        flags_t, group_precision * left_dot(flags, field)
    )


def pack_kernel(b, d, gi, w1, ac, w2, gc, w3, out, turned):
    own = lax.axis_index("x") * 8 + lax.axis_index("z")
    for i in range(8):
        turned[pl.ds(i, 128, stride=8), :] = b[i * 128 : (i + 1) * 128, :].T
    d_flat = jnp.concatenate([d[pl.ds(k, 8, stride=4), :] for k in range(4)], axis=1)
    w1_flat = jnp.concatenate([w1[k : k + 1, :] for k in range(4)], axis=1)
    gi_turned = gi[...].T
    mine = (iota((4, 32, 128), 1) == own).astype(F32)
    corner = jnp.sum(gc[...] * mine, axis=1)
    corner_weight = jnp.sum(
        jnp.where(iota((4, 32), 1) == own, w3[...], 0.0), axis=1, keepdims=True
    )
    row, lane = iota((32, 128), 0), iota((32, 128), 1)
    place = ((row % 4 == lane // 32) & (row // 4 == lane % 8)).astype(F32)
    w2_row = jnp.sum(w2[...] * place, axis=0, keepdims=True)
    row, lane = iota((4, 128), 0), iota((4, 128), 1)
    place_corner = ((lane < 16) & (lane // 4 == row)).astype(F32)
    w3_row = jnp.sum(
        corner_weight * ((lane >= 16) & (lane < 32) & (lane // 4 - 4 == row)).astype(F32),
        axis=0,
        keepdims=True,
    )
    dims = (((0,), (0,)), ((), ()))
    row, lane = iota((128, 128), 0), iota((128, 128), 1)
    a = lax.dot_general(ac[...], place, dims, precision=HIGH, preferred_element_type=F32)
    a = jnp.where(row % 4 == (lane // 8) % 4, a, 0.0)
    z = lax.dot_general(
        corner * corner_weight, place_corner, dims, precision=HIGH, preferred_element_type=F32
    )
    z = jnp.where(row % 4 == lane % 4, z, 0.0)
    fold = (iota((32, 128), 1) // 4 == iota((32, 128), 0)).astype(F32)
    a = jnp.dot(fold, a, precision=HIGH, preferred_element_type=F32) * w2_row
    z = jnp.dot(fold, z, precision=HIGH, preferred_element_type=F32) + w3_row
    for s in range(32):
        out[s, 0:32, :] = turned[s * 32 : (s + 1) * 32, :]
        out[s, 32:40, :] = d_flat
        out[s, 40:44, :] = gi_turned[s * 4 : (s + 1) * 4, :]
        out[s, 44:45, :] = w1_flat
        out[s, 45:46, :] = a[s : s + 1, :]
        out[s, 46:47, :] = w2_row
        out[s, 47:48, :] = z[s : s + 1, :]


def spread_kernel(
    got, kap, gam, out, field_out, d_out, w1_out, flags_out, flags_t_out, own_out, s_ref, y_ref
):
    lane4 = iota((4, 128), 1)
    corner, corner_weight = jnp.zeros((4, 128), F32), jnp.zeros((4, 128), F32)
    own_out[...] = jnp.zeros_like(own_out)
    for g in range(8):
        pieces = swapped([got[g * 4 + x] for x in range(4)])
        for k in range(4):
            piece = pieces[k]
            d_out[(g * 4 + k) * 8 : (g * 4 + k + 1) * 8, :] = piece[32:40]
            for h in range(4):
                at = g * 128 + k * 32 + h * 8
                s_ref[at : at + 8, :] = piece[h * 8 : (h + 1) * 8] * piece[32:40]
            at = g * 16 + k * 4
            y_ref[at : at + 4, :] = piece[40:44] * piece[44:45]
            w1_out[at : at + 4, :] = jnp.broadcast_to(piece[44:45], (4, 128))
        lanes = slice(g * 128, (g + 1) * 128)
        z = jnp.concatenate([got[g * 4 + x, 47:48, :] for x in range(4)], axis=0)
        corner += pltpu.roll(jnp.where(lane4 < 16, z, 0.0), g * 16, 1)
        corner_weight += pltpu.roll(
            jnp.where((lane4 >= 16) & (lane4 < 32), z, 0.0), (g * 16 + 112) % 128, 1
        )
        for x in range(4):
            own_out[x : x + 1, lanes] = got[g * 4 + x, 45:46, :]
            own_out[8 + x : 9 + x, lanes] = got[g * 4 + x, 46:47, :]
    flags32 = (iota((128, 1024), 0) == kap[...]).astype(F32)
    flags, flags_t = flags32.astype(BF16), flags32.T.astype(BF16)
    flags_out[...] = flags
    flags_t_out[...] = flags_t
    own_out[0:4, :] += right_dot(corner, flags)
    own_out[16:20, 0:128] = corner_weight
    c0, c1 = class_flags(gam[...])
    w1, d = w1_out[...], d_out[...]
    field = s_ref[...] + left_dot(flags_t, y_ref[...])
    field_out[...] = field
    y0 = own_out[0:8, :]
    total = over_lanes(c0, field)
    field = region_mix(field, d, w1, flags, flags_t)
    total += over_lanes(c1, field)
    field = region_mix(field, d, w1, flags, flags_t)
    last = over_lanes(c0, field)
    y0 = pltpu.roll(y0, 4, 0)
    members = jnp.sum(flags32, axis=1, keepdims=True)
    w1_lifted = left_dot(flags_t, w1).reshape(32, 4, 8, 128)[:, 0].reshape(256, 128)
    small = []
    for v in (d, d * d, d * w1_lifted):
        small.append(over_lanes(c0, v[0:128]) + over_lanes(c1, v[128:256]))
    small.append(over_lanes(c0, w1) + over_lanes(c1, members * w1 * w1))
    for z in range(8):
        rows = slice(z * 8, (z + 1) * 8)
        for t in range(8):
            lanes = slice(t * 128, (t + 1) * 128)
            out[z, t * 8 : (t + 1) * 8, :] = total[rows, lanes]
            out[z, 64 + t * 8 : 64 + (t + 1) * 8, :] = last[rows, lanes] + y0[:, lanes]
        for j in range(4):
            out[z, 128 + j * 8 : 128 + (j + 1) * 8, :] = small[j][rows]


def stacked(ref, first):
    rows = [
        jnp.concatenate(
            [ref[z, first + t * 8 : first + (t + 1) * 8, :] for t in range(8)], axis=1
        )
        for z in range(8)
    ]
    return jnp.concatenate(rows, axis=0)


def row_sums(value):
    rows = jnp.sum(value, axis=0, keepdims=True)
    return sum(rows[:, t * 128 : (t + 1) * 128] for t in range(value.shape[1] // 128))


def middle_kernel(
    got, field_in, d_in, w1_in, flags_in, flags_t_in, own, sizes, gam, out, r0_out, br_out
):
    flags, flags_t, d, w1 = flags_in[...], flags_t_in[...], d_in[...], w1_in[...]
    top = iota((8, 1024), 0) < 4
    top_small = iota((8, 128), 0) < 4

    def upper(value):
        return jnp.where(top if value.shape[1] == 1024 else top_small, value, 0.0)

    def lower(value):
        return upper(pltpu.roll(value, 4, 0))

    def row(first):
        return jnp.concatenate(
            [
                sum(got[z, first + t * 8 : first + (t + 1) * 8, :] for z in range(8))
                for t in range(8)
            ],
            axis=1,
        )

    small = [sum(got[z, 128 + j * 8 : 136 + j * 8, :] for z in range(8)) for j in range(4)]
    tile_row, tile_lane = iota((128, 1024), 0), iota((128, 1024), 1)
    from_at = (tile_lane // 32) * 8 + tile_lane % 8
    first = (from_at == tile_row).astype(F32).astype(BF16)
    second = (from_at == tile_row + 128).astype(F32).astype(BF16)
    wide = right_dot(jnp.concatenate([upper(v) for v in small[:3]], axis=0), first)
    wide += right_dot(jnp.concatenate([lower(v) for v in small[:3]], axis=0), second)
    vd, vd2, e = wide[0:8], wide[8:16], wide[16:24]
    vw, vw2 = upper(small[3]), lower(small[3])
    v01, v2 = row(0), upper(row(64))
    v0, v1 = upper(v01), lower(v01)
    y0, w2, w3 = own[0:8, :], own[8:16, :], own[16:24, 0:128]
    n = jnp.concatenate([sizes[...]] * 8, axis=1)

    def up(value):
        return right_dot(value, flags_t)

    def down(value):
        return right_dot(value, flags)

    def shared(value):
        return w2 * value + down(w3 * up(value))

    sums = up(jnp.concatenate([y0, e * y0], axis=0))
    u0, ue = sums[0:8], sums[8:16]
    lifts = down(jnp.concatenate([u0, vw * u0, ue + vw2 * u0], axis=0))
    b1 = v1 + vd * y0 + lifts[8:16]
    b2 = v2 + vd2 * y0 + e * lifts[0:8] + lifts[16:24]
    g0 = v0 + n * y0
    y1 = shared(g0)
    g1 = b1 + n * y1
    y2 = shared(g1)
    k1 = vd * y1 + down(vw * up(y1))
    m1 = row_sums(g0 * y1)
    m2 = row_sums((2.0 * b1 + n * y1) * y1)
    m3 = row_sums((2.0 * b2 + k1) * y1 + g1 * y2)

    _, c1 = class_flags(gam[...])
    r0 = field_in[...] + over_rows(stacked(got, 64), c1)
    r0_out[...] = r0
    br = region_mix(r0, d, w1, flags, flags_t)
    br_out[...] = br
    bbr = region_mix(br, d, w1, flags, flags_t)
    m0 = row_sums(r0 * r0)
    m1 += row_sums(r0 * br)
    m2 += row_sums(br * br)
    m3 += row_sums(br * bbr)
    moments = jnp.concatenate([m0, m1, m2, m3, jnp.zeros((4, 128), F32)], axis=0)
    both = y1 + pltpu.roll(y2, 4, 0)
    for z in range(8):
        for t in range(8):
            out[z, t * 8 : (t + 1) * 8, :] = both[:, t * 128 : (t + 1) * 128]
        out[z, 64:72, :] = moments


def fields_kernel(got, r0_in, br_in, d_in, w1_in, flags_in, flags_t_in, gam, out, f_ref, g_ref):
    c0, c1 = class_flags(gam[...])
    shares = stacked(got, 0)
    field = br_in[...] + over_rows(shares, c0)
    f_ref[...] = field
    g_ref[...] = region_mix(
        field, d_in[...], w1_in[...], flags_in[...], flags_t_in[...]
    ) + over_rows(shares, c1)
    moments = sum(got[z, 64:72, :] for z in range(8))
    for g in range(8):
        for i, ref in enumerate((r0_in, f_ref, g_ref)):
            pieces = swapped([ref[g * 128 + k * 32 : g * 128 + (k + 1) * 32, :] for k in range(4)])
            for x in range(4):
                out[g * 4 + x, i * 32 : (i + 1) * 32, :] = pieces[x]
        for x in range(4):
            out[g * 4 + x, 96:104, :] = moments


def finish_kernel(got, x_out, r_out, x_ref, r_ref):
    tile = got[0, 96:104, :]
    for s in range(1, 32):
        tile += got[s, 96:104, :]
    m = jnp.sum(tile, axis=1, keepdims=True)
    m0, m1, m2, m3 = (m[i : i + 1, :] for i in range(4))
    alpha = m0 / m1
    norm = m0 - 2.0 * alpha * m1 + alpha * alpha * m2
    grown = 1.0 + norm / m0
    product = grown * grown * m1 - 2.0 * grown * alpha * m2 + alpha * alpha * m3
    later = norm / product
    on_first, on_second = alpha + later * grown, -later * alpha
    for s in range(32):
        first, second, third = got[s, 0:32, :], got[s, 32:64, :], got[s, 64:96, :]
        x_ref[s * 32 : (s + 1) * 32, :] = on_first * first + on_second * second
        r_ref[s * 32 : (s + 1) * 32, :] = first - on_first * second - on_second * third
    for i in range(8):
        x_out[i * 128 : (i + 1) * 128, :] = x_ref[pl.ds(i, 128, stride=8), :].T
        r_out[i * 128 : (i + 1) * 128, :] = r_ref[pl.ds(i, 128, stride=8), :].T


def call(kernel, outs, scratch=()):
    vmem = pl.BlockSpec(memory_space=pltpu.VMEM)
    return lambda *args: pl.pallas_call(
        kernel,
        out_shape=tuple(jax.ShapeDtypeStruct(shape, kind) for shape, kind in outs),
        in_specs=[vmem] * len(args),
        out_specs=(vmem,) * len(outs),
        scratch_shapes=[pltpu.VMEM(shape, F32) for shape in scratch],
    )(*args)


def exchanged(value, axes):
    return lax.all_to_all(value, axes, 0, 0, tiled=True)


def row_of(table, wanted, names):
    hit = table[:, :, None] == wanted[None, None, :]
    return jnp.sum(jnp.where(hit, names[:, None, None], 0), axis=(0, 1), dtype=jnp.int32)


def on_device(b, gi, ac, gc, d, w1, w2, w3, group_table, class_table):
    z = lax.axis_index("z")
    (sent,) = call(pack_kernel, [((32, 48, 128), F32)], [(1024, 128)])(
        b.reshape(1024, 128), d, gi.reshape(128, 128), w1, ac.reshape(32, 128), w2, gc, w3
    )
    got = exchanged(sent, SPLIT)

    parent = row_of(group_table, jnp.arange(256, dtype=jnp.int32), jnp.arange(32, dtype=jnp.int32))
    kap = parent.reshape(8, 8, 4).transpose(0, 2, 1)[:, :, None, :] * 4
    kap = (kap + jnp.arange(4, dtype=jnp.int32)[None, None, :, None]).reshape(1, 1024)
    lane = jnp.arange(128, dtype=jnp.int32)
    category = jnp.arange(32, dtype=jnp.int32)
    gam = row_of(
        class_table,
        (lane // 32) * 256 + z * 32 + lane % 32,
        (category % 8) * 4 + category // 8,
    ).reshape(1, 128)
    count = jnp.sum((class_table >= 0).astype(F32), axis=1).reshape(4, 8)
    count = jnp.sum(jnp.where(jnp.arange(8)[None, :] == z, count, 0.0), axis=1)
    sizes = jnp.broadcast_to(jnp.pad(count, (0, 4))[:, None], (8, 128))

    sent, field, d_all, w1_all, flags, flags_t, own = call(
        spread_kernel,
        [
            ((8, 160, 128), F32),
            ((1024, 128), F32),
            ((256, 128), F32),
            ((128, 128), F32),
            ((128, 1024), BF16),
            ((1024, 128), BF16),
            ((24, 1024), F32),
        ],
        [(1024, 128), (128, 128)],
    )(got, kap, gam)
    got = exchanged(sent, "z")
    sent, r0, br = call(
        middle_kernel, [((8, 72, 128), F32), ((1024, 128), F32), ((1024, 128), F32)]
    )(got, field, d_all, w1_all, flags, flags_t, own, sizes, gam)
    got = exchanged(sent, "z")
    (sent,) = call(fields_kernel, [((32, 104, 128), F32)], [(1024, 128), (1024, 128)])(
        got, r0, br, d_all, w1_all, flags, flags_t, gam
    )
    got = exchanged(sent, SPLIT)
    solution_field, residual = call(
        finish_kernel, [((1024, 128), F32)] * 2, [(1024, 128), (1024, 128)]
    )(got)
    return solution_field.reshape(32, 32, 128), residual.reshape(32, 32, 128)


def solution(mesh):
    finer = Mesh(mesh.devices.reshape(4, 2, 4, 8), ("y", "core", "x", "z"))
    return jax.shard_map(
        on_device,
        mesh=finer,
        in_specs=(
            P(REG, PROD, None),
            P(REG, PROD, None),
            P(REG, PROD, None),
            P(REG, None, None),
            P(REG, PROD),
            P(REG, PROD),
            P(REG, PROD),
            P(REG, None),
            P(),
            P(),
        ),
        out_specs=(P(REG, PROD, None), P(REG, PROD, None)),
        check_vma=False,
    )
```

time: 311 us -> 124 us (0.40)
  waiting for transfers between devices: 104 us -> 31 us
  blocking collectives: 106 us -> 45.8 us
  starting transfers between devices: 62.4 us -> 16.8 us
  Pallas kernels: 0 us -> 22.9 us
  local copies, waits for them, and re-layouts: 15.6 us -> 4.09 us
  matrix products: 9.88 us -> 0 us
  between operations: 6.77 us -> 0.72 us
    all_to_all x10 -> x2, waiting for transfers between devices: 104 us -> 31 us  [exchanged(): return lax.all_to_all(value, axes, 0, 0, tiled=True)]
    all_to_all x8 -> x2, blocking collectives: 106 us -> 45.8 us  [exchanged(): return lax.all_to_all(value, axes, 0, 0, tiled=True)]
    all_to_all x10 -> x2, starting transfers between devices: 62.4 us -> 16.8 us  [exchanged(): return lax.all_to_all(value, axes, 0, 0, tiled=True)]
    pallas_call x0 -> x5, Pallas kernels: none -> 22.9 us  [call(): pl.pallas_call(kernel, out_shape=tuple((jax.ShapeDtypeStruct(shape, kind)...]
    dot_general x15 -> x0, matrix products: 9.88 us -> none  [the longest x3 3.56 us: disaggregate_onto(): jnp.einsum('pr,pqh->rqh', block, gathered_copies(upper, REG, 0), precisio...]
    broadcast_in_dim x12 -> x1, local copies, waits for them, and re-layouts: 6.46 us -> 0.74 us  [on_device(): sizes = jnp.broadcast_to(jnp.pad(count, (0, 4))[:, None], (8, 128))]
  transfers between devices with their start and end apart: 10 -> 2, of which waited for: 10 -> 2; matrix products, arithmetic and copies ran while one was open for 2% -> 3% of each run, Pallas kernels for 0% -> 0%
where the time goes in v1:
time: 124 us
  blocking collectives  45.8 us (37%)
  waiting for transfers between devices  31 us (25%)
  Pallas kernels  22.9 us (18%)
  starting transfers between devices  16.8 us (14%)
  local copies, waits for them, and re-layouts  4.09 us (3%)
  other arithmetic  2.32 us (2%)
    all_to_all x2, blocking collectives, exchanged(): return lax.all_to_all(value, axes, 0, 0, tiled=True)  45.8 us
    all_to_all x2, waiting for transfers between devices, exchanged(): return lax.all_to_all(value, axes, 0, 0, tiled=True)  31 us
    pallas_call x5, Pallas kernels, call(): pl.pallas_call(kernel, out_shape=tuple((jax.ShapeDtypeStruct(shape, kind)...  22.9 us
    all_to_all x2, starting transfers between devices, exchanged(): return lax.all_to_all(value, axes, 0, 0, tiled=True)  16.8 us
  transfers between devices with their start and end apart: 2, of which 2 were waited for; matrix products, arithmetic and copies ran while one was open for 3% of the time, Pallas kernels for 0%

profile of v1, /device:TPU:1, one launch (start us, length us, event | category | flops | bytes accessed | tf_op | source)
XLA Modules:
  0.0 123.6 jit_solution(9395406081738751372)
XLA Ops:
  0.6 0.0 copy-start.3
  0.6 0.0 copy-start.2
  0.7 1.4 %copy.15.w2 = f32[32,1]{1,0:T(8,128)} copy(f32[32,1]{0,1:T(1,128)} %param.16) | data formatting | bytes 256 | tf_op args[6]
  2.0 2.6 %shard_map.113 = f32[32,48,128]{2,1,0:T(8,128)} custom-call(f32[1024,128]{1,0:T(8,128)} %bitcast.7, f32[32,32]{1,0:T(8,128)} %d.1, f32[128,128]{1,0:T(8,128)} %bitcast.9, f32[4,32]{1,0:T(4,128)} %w1.1, f32[32,128]{1,0:T(8,128)} %bitcast.10, f32[32,1]{1,0:T(8,128)} %copy.15.w2, f32[4,32,128]{2,1,0:T(8,128)} %gc.1, f32[4,32]{1,0:T(4,128)} %w3.1), custom_call_target="tpu_custom_call" | custom-call | tf_op jit(solution)/shard_map/pallas_call | solution.py:317
  4.6 8.6 %all-to-all-start = ((f32[32,48,128]{2,1,0:T(8,128)}), f32[32,48,128]{2,1,0:T(8,128)S(1)}, u32[]{:S(2)}, u32[]{:S(2)}) async-start(f32[32,48,128]{2,1,0:T(8,128)} %shard_map.113), calls=%async_computation | async-start | bytes 1572864 | tf_op jit(solution)/shard_map/all_to_all | solution.py:327
  13.2 0.0 copy-done.3
  13.2 0.7 select_reduce_fusion
  13.9 0.1 mul.38
  14.1 0.1 copy.16
  14.2 0.7 add.82.kap
  14.9 0.0 copy-done.2
  14.9 1.3 %select_reduce_fusion.1 = s32[128]{0:T(128)} fusion(s32[32]{0:T(128)S(1)} %fusion.2, s32[128]{0:T(128)S(1)} %fusion, s32[32,128]{1,0:T(8,128)S(1)} %copy-done.2), kind=kLoop, calls=%fused_computation.2 | loop fusion | flops 1572736 | bytes 17536 | tf_op jit(solution)/shard_map/reduce_sum | solution.py:332
  16.3 10.6 %all-to-all-done.got = f32[32,48,128]{2,1,0:T(8,128)S(1)} async-done(((f32[32,48,128]{2,1,0:T(8,128)}), f32[32,48,128]{2,1,0:T(8,128)S(1)}, u32[]{:S(2)}, u32[]{:S(2)}) %all-to-all-start) | async-done | bytes 786464 | tf_op jit(solution)/shard_map/all_to_all | solution.py:327
  26.9 0.0 copy-start
  26.9 0.9 copy-done
  27.8 6.4 %shard_map.114 = (f32[8,160,128]{2,1,0:T(8,128)}, f32[1024,128]{1,0:T(8,128)}, f32[256,128]{1,0:T(8,128)}, f32[128,128]{1,0:T(8,128)}, bf16[128,1024]{1,0:T(8,12...) custom-call(f32[32,48,128]{2,1,0:T(8,128)} %copy-done, s32[1,1024]{1,0:T(1,128)} %add.82.kap, s32[1,128]{1,0:T(1,128)} %bitcast.11), custom_call_target="tpu_custom_call" | custom-call | tf_op jit(solution)/shard_map/pallas_call | solution.py:317
  34.2 8.2 %all-to-all-start.1 = ((f32[8,160,128]{2,1,0:T(8,128)}), f32[8,160,128]{2,1,0:T(8,128)S(1)}, u32[]{:S(2)}, u32[]{:S(2)}) async-start(f32[8,160,128]{2,1,0:T(8,128)} %get-tuple-element.14), calls=%async_computation.1 | async-start | bytes 1310720 | tf_op jit(solution)/shard_map/all_to_all | solution.py:327
  42.4 0.1 convert_reduce_fusion
  42.5 0.1 reshape.110
  42.6 0.1 select_reduce_fusion.2
  42.7 20.4 %all-to-all-done.1.got = f32[8,160,128]{2,1,0:T(8,128)S(1)} async-done(((f32[8,160,128]{2,1,0:T(8,128)}), f32[8,160,128]{2,1,0:T(8,128)S(1)}, u32[]{:S(2)}, u32[]{:S(2)}) %all-to-all-start.1) | async-done | bytes 655392 | tf_op jit(solution)/shard_map/all_to_all | solution.py:327
  63.1 0.0 copy-start.1
  63.1 0.7 broadcast_in_dim.57.sizes
  63.9 0.1 copy-done.1
  64.0 6.2 %shard_map.115 = (f32[8,72,128]{2,1,0:T(8,128)}, f32[1024,128]{1,0:T(8,128)}, f32[1024,128]{1,0:T(8,128)}) custom-call(f32[8,160,128]{2,1,0:T(8,128)} %copy-done.1, f32[1024,128]{1,0:T(8,128)} %get-tuple-element.15.field_in, f32[256,128]{1,0:T(8,128)} %get-tuple-element.16.d_in, f32[128,128]{1,0:T(8,128)} %get-tuple-element.17.w1_in, ...), custom_call_target="tpu_custom_call" | custom-call | tf_op jit(solution)/shard_map/pallas_call | solution.py:317
  70.1 16.8 %all_to_all.20.got = f32[8,72,128]{2,1,0:T(8,128)} all-to-all(f32[8,72,128]{2,1,0:T(8,128)} %get-tuple-element.21), channel_id=1, replica_groups=mesh['y'=4,'core'=2,'x'=4,'z'=8] {'z'}, dimensions={0} | all-to-all | bytes 589824 | tf_op jit(solution)/shard_map/all_to_all | solution.py:327
  86.9 4.6 %shard_map.116 = f32[32,104,128]{2,1,0:T(8,128)} custom-call(f32[8,72,128]{2,1,0:T(8,128)} %all_to_all.20.got, f32[1024,128]{1,0:T(8,128)} %get-tuple-element.22.r0_in, f32[1024,128]{1,0:T(8,128)} %get-tuple-element.23.br_in, f32[256,128]{1,0:T(8,128)} %get-tuple-element.16.d_in, f32[128,128]{1,0:T(8,128)} %get-tuple-element.17.w1_in, ...), custom_call_target="tpu_custom_call" | custom-call | tf_op jit(solution)/shard_map/pallas_call | solution.py:317
  91.5 29.0 %all_to_all.21.got = f32[32,104,128]{2,1,0:T(8,128)} all-to-all(f32[32,104,128]{2,1,0:T(8,128)} %shard_map.116), channel_id=1, replica_groups=mesh['y'=4,'core'=2,'x'=4,'z'=8] {'y','core','x'}, dimensions={0} | all-to-all | bytes 3407872 | tf_op jit(solution)/shard_map/all_to_all | solution.py:327
  120.5 3.1 %shard_map.117 = (f32[1024,128]{1,0:T(8,128)}, f32[1024,128]{1,0:T(8,128)}) custom-call(f32[32,104,128]{2,1,0:T(8,128)} %all_to_all.21.got), custom_call_target="tpu_custom_call" | custom-call | tf_op jit(solution)/shard_map/pallas_call | solution.py:317
  (6 shorter events, 0.0 us)
Async XLA Ops:
  0.6 12.6 %copy-start.3 = (s32[32,128]{1,0:T(8,128)S(1)}, s32[32,128]{1,0:T(8,128)}, u32[]{:S(2)}) copy-start(s32[32,128]{1,0:T(8,128)} %param.18) | copy-start | bytes 49156
  0.6 14.3 %copy-start.2 = (s32[32,128]{1,0:T(8,128)S(1)}, s32[32,128]{1,0:T(8,128)}, u32[]{:S(2)}) copy-start(s32[32,128]{1,0:T(8,128)} %param.19) | copy-start | bytes 49156
  4.6 22.3 %all-to-all-start = ((f32[32,48,128]{2,1,0:T(8,128)}), f32[32,48,128]{2,1,0:T(8,128)S(1)}, u32[]{:S(2)}, u32[]{:S(2)}) async-start(f32[32,48,128]{2,1,0:T(8,128)} %shard_map.113), calls=%async_computation | async-start | bytes 1572864 | tf_op jit(solution)/shard_map/all_to_all | solution.py:327
  26.9 0.9 copy-start
  34.2 28.9 %all-to-all-start.1 = ((f32[8,160,128]{2,1,0:T(8,128)}), f32[8,160,128]{2,1,0:T(8,128)S(1)}, u32[]{:S(2)}, u32[]{:S(2)}) async-start(f32[8,160,128]{2,1,0:T(8,128)} %get-tuple-element.14), calls=%async_computation.1 | async-start | bytes 1310720 | tf_op jit(solution)/shard_map/all_to_all | solution.py:327
  63.1 0.8 copy-start.1

commit v2 on v0

v2 whole, which is shorter than its diff:
```python
import jax
import jax.numpy as jnp
from jax import lax
from jax.experimental import pallas as pl
from jax.experimental.pallas import tpu as pltpu
from jax.sharding import Mesh
from jax.sharding import PartitionSpec as P

F32 = jnp.float32
BF16 = jnp.bfloat16
REG = ("y", "core")
PROD = ("x", "z")
SPLIT = ("y", "core", "x")
LANES = (((1,), (1,)), ((), ()))


def iota(shape, dim):
    return lax.broadcasted_iota(jnp.int32, shape, dim)


def flag(condition):
    return condition.astype(F32).astype(BF16)


def parts(value):
    high = value.astype(BF16)
    return high, (value - high.astype(F32)).astype(BF16)


def dot(a, b):
    if a.dtype == BF16:
        return sum(jnp.dot(a, p, preferred_element_type=F32) for p in parts(b))
    return sum(jnp.dot(p, b, preferred_element_type=F32) for p in parts(a))


def dot_t(value, flags):
    return sum(lax.dot_general(p, flags, LANES, preferred_element_type=F32) for p in parts(value))


def swapped(pieces):
    group = iota(pieces[0].shape, 1) // 32
    odd, upper = (group & 1) == 1, group >= 2
    a = []
    for i in (0, 2):
        a.append(jnp.where(odd, pltpu.roll(pieces[i + 1], 32, 1), pieces[i]))
        a.append(jnp.where(odd, pieces[i + 1], pltpu.roll(pieces[i], 96, 1)))
    return (
        jnp.where(upper, pltpu.roll(a[2], 64, 1), a[0]),
        jnp.where(upper, pltpu.roll(a[3], 64, 1), a[1]),
        jnp.where(upper, a[2], pltpu.roll(a[0], 64, 1)),
        jnp.where(upper, a[3], pltpu.roll(a[1], 64, 1)),
    )


def group_flags(parent):
    row = iota((128, 256), 0)
    return [flag(row == parent + 32 * h) for h in range(4)]


def category_flags(places):
    row = iota((128, 128), 0)
    return [flag(row == places * 4 + h) for h in range(4)]


def grouped(field, flags):
    return sum(dot_t(field[h], flags[h]) for h in range(4))


def ungrouped(value, flags):
    high, low = parts(value)
    return [
        jnp.dot(high, f, preferred_element_type=F32) + jnp.dot(low, f, preferred_element_type=F32)
        for f in flags
    ]


def mixed(field, precision, group_precision, flags):
    lifted = ungrouped(group_precision * grouped(field, flags), flags)
    return [precision * field[h] + lifted[h] for h in range(4)]


def categories(field, flags):
    return sum(dot(flags[h], field[h]) for h in range(4))


def lifted_categories(value, flags):
    high, low = parts(value)
    dims = (((0,), (0,)), ((), ()))
    return [
        lax.dot_general(f, high, dims, preferred_element_type=F32)
        + lax.dot_general(f, low, dims, preferred_element_type=F32)
        for f in flags
    ]


def steps(ref):
    return [ref[h * 128 : (h + 1) * 128, :] for h in range(4)]


def pack_kernel(b, d, gi, w1, ac, w2, gc, w3, out, turned, turned_small):
    own = lax.axis_index("x") * 8 + lax.axis_index("z")
    for i in range(8):
        block = jnp.concatenate(
            [b[pl.ds(k * 8 + i, 32, stride=32), :] for k in range(4)], axis=0
        )
        turned[pl.ds(i, 128, stride=8), :] = block.T
    d_turned = d[...].T
    d_rows = jnp.concatenate([d_turned[k * 8 : (k + 1) * 8] for k in range(4)], axis=1)
    w1_row = jnp.concatenate([w1[k : k + 1, :] for k in range(4)], axis=1)
    w2_row = jnp.concatenate([w2[...]] * 4, axis=1)
    gi_turned = gi[...].T
    mine = (iota((4, 32, 128), 1) == own).astype(F32)
    corner = jnp.sum(gc[...] * mine, axis=1)
    weight = jnp.sum(jnp.where(iota((4, 32), 1) == own, w3[...], 0.0), axis=1, keepdims=True)
    small = [ac[...], corner * weight, jnp.broadcast_to(weight, (4, 128))]
    small = jnp.concatenate([*small, jnp.zeros((88, 128), F32)], axis=0)
    turned_small[...] = small.T
    values = [turned_small[pl.ds(h, 32, stride=4), :] for h in range(4)]
    a = jnp.concatenate([v[:, 0:32] for v in values], axis=1) * w2_row
    z = jnp.concatenate([v[:, 32:64] for v in values], axis=1)
    for s in range(32):
        out[s, 0:32, :] = turned[s * 32 : (s + 1) * 32, :]
        out[s, 32:40, :] = d_rows
        out[s, 40:44, :] = gi_turned[s * 4 : (s + 1) * 4, :]
        out[s, 44:45, :] = w1_row
        out[s, 45:46, :] = a[s : s + 1, :]
        out[s, 46:47, :] = w2_row
        out[s, 47:48, :] = z[s : s + 1, :]


def spread_kernel(got, parent, gam, table, out, field_out, d_out, w1_out, own_out, g_ref, k_ref):
    for x in range(4):
        for half in range(2):
            lanes = slice(half * 128, (half + 1) * 128)
            pieces = swapped([got[(half * 4 + g) * 4 + x] for g in range(4)])
            for k in range(4):
                piece = pieces[k]
                at = x * 32 + k * 8
                d_out[at : at + 8, lanes] = piece[32:40]
                for h in range(4):
                    field_out[h * 128 + at : h * 128 + at + 8, lanes] = (
                        piece[h * 8 : (h + 1) * 8] * piece[32:40]
                    )
                for i in range(3):
                    own_out[i * 16 + x * 4 + k : i * 16 + x * 4 + k + 1, lanes] = piece[
                        45 + i : 46 + i
                    ]
    for g in range(8):
        pieces = swapped([got[g * 4 + x, 40:48, :] for x in range(4)])
        for k in range(4):
            g_ref[pl.ds(g * 4 + k, 4, stride=32), :] = pieces[k][0:4] * pieces[k][4:5]
            k_ref[pl.ds(g * 4 + k, 4, stride=32), :] = jnp.broadcast_to(
                pieces[k][4:5], (4, 128)
            )
    w1 = k_ref[...].T
    w1_out[...] = w1
    groups = group_flags(parent[...])
    flags = category_flags(gam[...])
    lane = iota((256, 256), 0)
    at = parent[...] // 4 * 32 + parent[...] % 4
    y0 = own_out[0:16, :] + dot(own_out[32:48, :], flag(lane == at))
    own_out[0:16, :] = y0
    d = d_out[...]
    lifted = ungrouped(g_ref[...].T, groups)
    field = [field_out[h * 128 : (h + 1) * 128, :] + lifted[h] for h in range(4)]
    for h in range(4):
        field_out[h * 128 : (h + 1) * 128, :] = field[h]
    totals = [categories(field, flags)]
    for _ in range(2):
        field = mixed(field, d, w1, groups)
        totals.append(categories(field, flags))
    plain = flag(iota((32, 128), 0) == gam[...])
    everywhere = flag(iota((128, 256), 0) % 32 == parent[...])
    members = lax.dot_general(
        jnp.ones((8, 256), BF16), everywhere, LANES, preferred_element_type=F32
    )[0:1]
    lifted_w1 = dot(w1, groups[0])
    small = [dot(plain, v) for v in (d, d * d, d * lifted_w1)]
    row, lane = iota((128, 256), 0), iota((128, 256), 1)
    at = jnp.where(row < 32, row // 4 * 32 + row % 4, -16)
    small.append(
        dot(dot(plain, w1), flag(lane == at + 4))
        + dot(dot(plain, members * w1 * w1), flag(lane == at + 8))
    )
    count = jnp.sum((table[...] >= 0).astype(F32), axis=1, keepdims=True)
    count = jnp.where(iota((32, 1), 0) % 8 == lax.axis_index("z"), count, 0.0)
    for x in range(4):
        size = jnp.sum(count[x * 8 : (x + 1) * 8], axis=0, keepdims=True)
        own_out[48 + x * 4 : 52 + x * 4, :] = jnp.broadcast_to(size, (4, 256))
    for z in range(8):
        for i in range(3):
            out[z, i * 16 : (i + 1) * 16, :] = totals[i][z * 16 : (z + 1) * 16]
        out[z, 48:64, :] = y0
        for i in range(4):
            out[z, 64 + i * 4 : 68 + i * 4, :] = small[i][z * 4 : (z + 1) * 4]


def lane_sums(value):
    rows = jnp.sum(value, axis=0, keepdims=True)
    return sum(rows[:, t * 128 : (t + 1) * 128] for t in range(value.shape[1] // 128))


def field_product(a, b):
    return lane_sums(sum(a[h] * b[h] for h in range(4)))


def middle_kernel(got, field_in, d_in, w1_in, own, parent, gam, out, r0_out, br_out):
    total = sum(got[z, 0:48, :] for z in range(8))
    small = sum(got[z, 64:80, :] for z in range(8))
    v0, v1, v2 = (total[i * 16 : (i + 1) * 16] for i in range(3))

    def repeated(first):
        rows = [
            jnp.broadcast_to(small[first + x : first + x + 1], (4, 256)) for x in range(4)
        ]
        return jnp.concatenate(rows, axis=0)

    vd, vd2, e, vw = (repeated(i * 4) for i in range(4))
    vw2 = pltpu.roll(vw, 252, 1)
    y0, w2, w3, n = (own[i * 16 : (i + 1) * 16, :] for i in range(4))
    at = parent[...] // 4 * 32 + parent[...] % 4 + 4
    places = flag(iota((256, 256), 0) == at)

    def up(value):
        return dot_t(value, places)

    def down(value):
        return dot(value, places)

    def shared(value):
        return w2 * value + down(w3 * up(value))

    sums = up(jnp.concatenate([y0, e * y0], axis=0))
    u0, ue = sums[0:16], sums[16:32]
    lifts = down(jnp.concatenate([u0, vw * u0, ue + vw2 * u0], axis=0))
    b1 = v1 + vd * y0 + lifts[16:32]
    b2 = v2 + vd2 * y0 + e * lifts[0:16] + lifts[32:48]
    g0 = v0 + n * y0
    y1 = shared(g0)
    g1 = b1 + n * y1
    y2 = shared(g1)
    k1 = vd * y1 + down(vw * up(y1))
    m1 = lane_sums(g0 * y1)
    m2 = lane_sums((2.0 * b1 + n * y1) * y1)
    m3 = lane_sums((2.0 * b2 + k1) * y1 + g1 * y2)

    groups, flags, d, w1 = group_flags(parent[...]), category_flags(gam[...]), d_in[...], w1_in[...]
    shares = jnp.concatenate([got[z, 48:64, :] for z in range(8)], axis=0)
    lifted = lifted_categories(shares, flags)
    field = steps(field_in)
    r0 = [field[h] + lifted[h] for h in range(4)]
    br = mixed(r0, d, w1, groups)
    for h in range(4):
        r0_out[h * 128 : (h + 1) * 128, :] = r0[h]
        br_out[h * 128 : (h + 1) * 128, :] = br[h]
    rows = grouped(br, groups)
    m0 = field_product(r0, r0)
    m1 += field_product(r0, br)
    m2 += field_product(br, br)
    m3 += field_product(br, [d * v for v in br]) + lane_sums(w1 * rows * rows)
    moments = jnp.concatenate([m0, m1, m2, m3, jnp.zeros((4, 128), F32)], axis=0)
    for z in range(8):
        out[z, 0:16, :] = y1
        out[z, 16:32, :] = y2
        out[z, 32:40, 0:128] = moments
        out[z, 32:40, 128:256] = jnp.zeros((8, 128), F32)


def fields_kernel(got, r0_in, br_in, d_in, w1_in, parent, gam, out, f_ref, g_ref):
    groups, flags = group_flags(parent[...]), category_flags(gam[...])
    first = lifted_categories(
        jnp.concatenate([got[z, 0:16, :] for z in range(8)], axis=0), flags
    )
    second = lifted_categories(
        jnp.concatenate([got[z, 16:32, :] for z in range(8)], axis=0), flags
    )
    br = steps(br_in)
    field = [br[h] + first[h] for h in range(4)]
    after = mixed(field, d_in[...], w1_in[...], groups)
    for h in range(4):
        f_ref[h * 128 : (h + 1) * 128, :] = field[h]
        g_ref[h * 128 : (h + 1) * 128, :] = after[h] + second[h]
    moments = sum(got[z, 32:40, 0:128] for z in range(8))
    for x in range(4):
        for half in range(2):
            lanes = slice(half * 128, (half + 1) * 128)
            for i, ref in enumerate((r0_in, f_ref, g_ref)):
                pieces = []
                for k in range(4):
                    at = x * 32 + k * 8
                    pieces.append(
                        jnp.concatenate(
                            [ref[h * 128 + at : h * 128 + at + 8, lanes] for h in range(4)], axis=0
                        )
                    )
                pieces = swapped(pieces)
                for g in range(4):
                    out[(half * 4 + g) * 4 + x, i * 32 : (i + 1) * 32, :] = pieces[g]
            for g in range(4):
                out[(half * 4 + g) * 4 + x, 96:104, :] = moments


def finish_kernel(got, x_out, r_out, x_ref, r_ref):
    tile = got[0, 96:104, :]
    for s in range(1, 32):
        tile += got[s, 96:104, :]
    m = jnp.sum(tile, axis=1, keepdims=True)
    m0, m1, m2, m3 = (m[i : i + 1, :] for i in range(4))
    alpha = m0 / m1
    norm = m0 - 2.0 * alpha * m1 + alpha * alpha * m2
    grown = 1.0 + norm / m0
    product = grown * grown * m1 - 2.0 * grown * alpha * m2 + alpha * alpha * m3
    later = norm / product
    on_first, on_second = alpha + later * grown, -later * alpha
    for s in range(32):
        first, second, third = got[s, 0:32, :], got[s, 32:64, :], got[s, 64:96, :]
        x_ref[s * 32 : (s + 1) * 32, :] = on_first * first + on_second * second
        r_ref[s * 32 : (s + 1) * 32, :] = first - on_first * second - on_second * third
    for i in range(8):
        for ref, out in ((x_ref, x_out), (r_ref, r_out)):
            block = ref[pl.ds(i, 128, stride=8), :].T
            for k in range(4):
                out[pl.ds(k * 8 + i, 32, stride=32), :] = block[k * 32 : (k + 1) * 32]


def call(kernel, outs, scratch=()):
    vmem = pl.BlockSpec(memory_space=pltpu.VMEM)
    return lambda *args: pl.pallas_call(
        kernel,
        out_shape=tuple(jax.ShapeDtypeStruct(shape, F32) for shape in outs),
        in_specs=[vmem] * len(args),
        out_specs=(vmem,) * len(outs),
        scratch_shapes=[pltpu.VMEM(shape, F32) for shape in scratch],
    )(*args)


def exchanged(value, axes):
    return lax.all_to_all(value, axes, 0, 0, tiled=True)


def row_of(table, wanted, names):
    hit = table[:, :, None] == wanted[None, None, :]
    return jnp.sum(jnp.where(hit, names[:, None, None], 0), axis=(0, 1), dtype=jnp.int32)[None]


def on_device(b, gi, ac, gc, d, w1, w2, w3, group_table, class_table):
    (sent,) = call(pack_kernel, [(32, 48, 128)], [(1024, 128), (128, 128)])(
        b.reshape(1024, 128),
        d,
        gi.reshape(128, 128),
        w1,
        ac.reshape(32, 128),
        w2.reshape(1, 32),
        gc,
        w3,
    )
    got = exchanged(sent, SPLIT)
    category = jnp.arange(32, dtype=jnp.int32)
    lane = jnp.arange(128, dtype=jnp.int32)
    parent = row_of(group_table, jnp.arange(256, dtype=jnp.int32), category)
    gam = row_of(
        class_table,
        (lane // 32) * 256 + lax.axis_index("z") * 32 + lane % 32,
        (category % 8) * 4 + category // 8,
    )
    sent, field, d_all, w1_all, own = call(
        spread_kernel,
        [(8, 80, 256), (512, 256), (128, 256), (128, 128), (64, 256)],
        [(128, 128), (128, 128)],
    )(got, parent, gam, class_table)
    got = exchanged(sent, "z")
    sent, r0, br = call(middle_kernel, [(8, 40, 256), (512, 256), (512, 256)])(
        got, field, d_all, w1_all, own, parent, gam
    )
    got = exchanged(sent, "z")
    (sent,) = call(fields_kernel, [(32, 104, 128)], [(512, 256), (512, 256)])(
        got, r0, br, d_all, w1_all, parent, gam
    )
    got = exchanged(sent, SPLIT)
    solution_field, residual = call(
        finish_kernel, [(1024, 128)] * 2, [(1024, 128), (1024, 128)]
    )(got)
    return solution_field.reshape(32, 32, 128), residual.reshape(32, 32, 128)


def solution(mesh):
    finer = Mesh(mesh.devices.reshape(4, 2, 4, 8), ("y", "core", "x", "z"))
    return jax.shard_map(
        on_device,
        mesh=finer,
        in_specs=(
            P(REG, PROD, None),
            P(REG, PROD, None),
            P(REG, PROD, None),
            P(REG, None, None),
            P(REG, PROD),
            P(REG, PROD),
            P(REG, PROD),
            P(REG, None),
            P(),
            P(),
        ),
        out_specs=(P(REG, PROD, None), P(REG, PROD, None)),
        check_vma=False,
    )
```

time: 311 us -> 118 us (0.38)
  waiting for transfers between devices: 104 us -> 11 us
  starting transfers between devices: 62.4 us -> 8.59 us
  blocking collectives: 106 us -> 74.8 us
  Pallas kernels: 0 us -> 19 us
  local copies, waits for them, and re-layouts: 15.6 us -> 0.9 us
  matrix products: 9.88 us -> 0 us
  between operations: 6.77 us -> 0.69 us
    all_to_all x10 -> x1, waiting for transfers between devices: 104 us -> 11 us  [exchanged(): return lax.all_to_all(value, axes, 0, 0, tiled=True)]
    all_to_all x10 -> x1, starting transfers between devices: 62.4 us -> 8.59 us  [exchanged(): return lax.all_to_all(value, axes, 0, 0, tiled=True)]
    all_to_all x8 -> x3, blocking collectives: 106 us -> 74.8 us  [exchanged(): return lax.all_to_all(value, axes, 0, 0, tiled=True)]
    pallas_call x0 -> x5, Pallas kernels: none -> 19 us  [call(): pl.pallas_call(kernel, out_shape=tuple((jax.ShapeDtypeStruct(shape, F32)...]
    dot_general x15 -> x0, matrix products: 9.88 us -> none  [the longest x3 3.56 us: disaggregate_onto(): jnp.einsum('pr,pqh->rqh', block, gathered_copies(upper, REG, 0), precisio...]
    broadcast_in_dim x12 -> x0, local copies, waits for them, and re-layouts: 6.46 us -> none  [copy_for_each(): copies = jnp.broadcast_to(value, (lax.axis_size(axis), *value.shape))]
    unnamed x19 -> x6, local copies, waits for them, and re-layouts: 4.98 us -> 0.9 us
  transfers between devices with their start and end apart: 10 -> 1, of which waited for: 10 -> 1; matrix products, arithmetic and copies ran while one was open for 2% -> 2% of each run, Pallas kernels for 0% -> 0%
where the time goes in v2:
time: 118 us
  blocking collectives  74.8 us (63%)
  Pallas kernels  19 us (16%)
  waiting for transfers between devices  11 us (9%)
  starting transfers between devices  8.59 us (7%)
  other arithmetic  2.61 us (2%)
    all_to_all x3, blocking collectives, exchanged(): return lax.all_to_all(value, axes, 0, 0, tiled=True)  74.8 us
    pallas_call x5, Pallas kernels, call(): pl.pallas_call(kernel, out_shape=tuple((jax.ShapeDtypeStruct(shape, F32)...  19 us
    all_to_all x1, waiting for transfers between devices, exchanged(): return lax.all_to_all(value, axes, 0, 0, tiled=True)  11 us
    all_to_all x1, starting transfers between devices, exchanged(): return lax.all_to_all(value, axes, 0, 0, tiled=True)  8.59 us
    reduce_sum x2, other arithmetic, row_of(): jnp.sum(jnp.where(hit, names[:, None, None], 0), axis=(0, 1), dtype=jnp.i...  2.59 us
  transfers between devices with their start and end apart: 1, of which 1 were waited for; matrix products, arithmetic and copies ran while one was open for 2% of the time, Pallas kernels for 0%

profile of v2, /device:TPU:1, one launch (start us, length us, event | category | flops | bytes accessed | tf_op | source)
XLA Modules:
  0.0 117.6 jit_solution(4544838955836113339)
XLA Ops:
  0.6 0.0 copy-start.1
  0.6 0.0 copy-start.2
  0.7 2.5 %shard_map.113 = f32[32,48,128]{2,1,0:T(8,128)} custom-call(f32[1024,128]{1,0:T(8,128)} %bitcast.8, f32[32,32]{1,0:T(8,128)} %d.1, f32[128,128]{1,0:T(8,128)} %bitcast.9, f32[4,32]{1,0:T(4,128)} %w1.1, f32[32,128]{1,0:T(8,128)} %bitcast.13, f32[1,32]{1,0:T(1,128)} %bitcast.17, f32[4,32,128]{2,1,0:T(8,128)} %gc.1, f32[4,32]{1,0:T(4,128)} %w3.1), custom_call_target="tpu_custom_call" | custom-call | tf_op jit(solution)/shard_map/pallas_call | solution.py:328
  3.2 8.6 %all-to-all-start = ((f32[32,48,128]{2,1,0:T(8,128)}), f32[32,48,128]{2,1,0:T(8,128)S(1)}, u32[]{:S(2)}, u32[]{:S(2)}) async-start(f32[32,48,128]{2,1,0:T(8,128)} %shard_map.113), calls=%async_computation | async-start | bytes 1572864 | tf_op jit(solution)/shard_map/all_to_all | solution.py:338
  11.8 0.0 copy-done.1
  11.8 1.3 %select_reduce_fusion.1 = s32[128]{0:T(128)} fusion(s32[32]{0:T(128)S(1)} %fusion.2, s32[128]{0:T(128)S(1)} %fusion, s32[32,128]{1,0:T(8,128)S(1)} %copy-done.1), kind=kLoop, calls=%fused_computation.2 | loop fusion | flops 1572736 | bytes 17536 | tf_op jit(solution)/shard_map/reduce_sum | solution.py:343
  13.1 0.0 copy-done.2
  13.1 1.3 %select_reduce_fusion = s32[256]{0:T(256)} fusion(s32[32,128]{1,0:T(8,128)S(1)} %copy-done.2), kind=kLoop, calls=%fused_computation | loop fusion | flops 3145472 | bytes 17408 | tf_op jit(solution)/shard_map/reduce_sum | solution.py:343
  14.4 11.0 %all-to-all-done.got = f32[32,48,128]{2,1,0:T(8,128)S(1)} async-done(((f32[32,48,128]{2,1,0:T(8,128)}), f32[32,48,128]{2,1,0:T(8,128)S(1)}, u32[]{:S(2)}, u32[]{:S(2)}) %all-to-all-start) | async-done | bytes 786464 | tf_op jit(solution)/shard_map/all_to_all | solution.py:338
  25.5 0.0 copy-start
  25.5 0.9 copy-done
  26.4 4.2 %shard_map.114 = (f32[8,80,256]{2,1,0:T(8,128)}, f32[512,256]{1,0:T(8,128)}, f32[128,256]{1,0:T(8,128)}, f32[128,128]{1,0:T(8,128)}, f32[64,256]{1,0:T(8,128)}) custom-call(f32[32,48,128]{2,1,0:T(8,128)} %copy-done, s32[1,256]{1,0:T(1,128)} %bitcast.10, s32[1,128]{1,0:T(1,128)} %bitcast.14, s32[32,128]{1,0:T(8,128)} %table.1), custom_call_target="tpu_custom_call" | custom-call | tf_op jit(solution)/shard_map/pallas_call | solution.py:328
  30.6 27.3 %all_to_all.20.got = f32[8,80,256]{2,1,0:T(8,128)} all-to-all(f32[8,80,256]{2,1,0:T(8,128)} %get-tuple-element.12), channel_id=1, replica_groups=mesh['y'=4,'core'=2,'x'=4,'z'=8] {'z'}, dimensions={0} | all-to-all | bytes 1310720 | tf_op jit(solution)/shard_map/all_to_all | solution.py:338
  57.9 4.4 %shard_map.115 = (f32[8,40,256]{2,1,0:T(8,128)}, f32[512,256]{1,0:T(8,128)}, f32[512,256]{1,0:T(8,128)}) custom-call(f32[8,80,256]{2,1,0:T(8,128)} %all_to_all.20.got, f32[512,256]{1,0:T(8,128)} %get-tuple-element.13.field_in, f32[128,256]{1,0:T(8,128)} %get-tuple-element.14.d_in, f32[128,128]{1,0:T(8,128)} %get-tuple-element.15.w1_in, ...), custom_call_target="tpu_custom_call" | custom-call | tf_op jit(solution)/shard_map/pallas_call | solution.py:328
  62.4 14.0 %all_to_all.21.got = f32[8,40,256]{2,1,0:T(8,128)} all-to-all(f32[8,40,256]{2,1,0:T(8,128)} %get-tuple-element.17), channel_id=1, replica_groups=mesh['y'=4,'core'=2,'x'=4,'z'=8] {'z'}, dimensions={0} | all-to-all | bytes 655360 | tf_op jit(solution)/shard_map/all_to_all | solution.py:338
  76.3 4.2 %shard_map.116 = f32[32,104,128]{2,1,0:T(8,128)} custom-call(f32[8,40,256]{2,1,0:T(8,128)} %all_to_all.21.got, f32[512,256]{1,0:T(8,128)} %get-tuple-element.18.r0_in, f32[512,256]{1,0:T(8,128)} %get-tuple-element.19.br_in, f32[128,256]{1,0:T(8,128)} %get-tuple-element.14.d_in, f32[128,128]{1,0:T(8,128)} %get-tuple-element.15.w1_in, s32[1,256]{1,0:T(1,128)} %bitcast.12, ...), custom_call_target="tpu_custom_call" | custom-call | tf_op jit(solution)/shard_map/pallas_call | solution.py:328
  80.5 33.5 %all_to_all.22.got = f32[32,104,128]{2,1,0:T(8,128)} all-to-all(f32[32,104,128]{2,1,0:T(8,128)} %shard_map.116), channel_id=1, replica_groups=mesh['y'=4,'core'=2,'x'=4,'z'=8] {'y','core','x'}, dimensions={0} | all-to-all | bytes 3407872 | tf_op jit(solution)/shard_map/all_to_all | solution.py:338
  114.0 3.6 %shard_map.117 = (f32[1024,128]{1,0:T(8,128)}, f32[1024,128]{1,0:T(8,128)}) custom-call(f32[32,104,128]{2,1,0:T(8,128)} %all_to_all.22.got), custom_call_target="tpu_custom_call" | custom-call | tf_op jit(solution)/shard_map/pallas_call | solution.py:328
  (2 shorter events, 0.0 us)
Async XLA Ops:
  0.6 11.2 %copy-start.1 = (s32[32,128]{1,0:T(8,128)S(1)}, s32[32,128]{1,0:T(8,128)}, u32[]{:S(2)}) copy-start(s32[32,128]{1,0:T(8,128)} %table.1) | copy-start | bytes 49156
  0.6 12.5 %copy-start.2 = (s32[32,128]{1,0:T(8,128)S(1)}, s32[32,128]{1,0:T(8,128)}, u32[]{:S(2)}) copy-start(s32[32,128]{1,0:T(8,128)} %param.18) | copy-start | bytes 49156
  3.2 22.3 %all-to-all-start = ((f32[32,48,128]{2,1,0:T(8,128)}), f32[32,48,128]{2,1,0:T(8,128)S(1)}, u32[]{:S(2)}, u32[]{:S(2)}) async-start(f32[32,48,128]{2,1,0:T(8,128)} %shard_map.113), calls=%async_computation | async-start | bytes 1572864 | tf_op jit(solution)/shard_map/all_to_all | solution.py:338
  25.5 0.9 copy-start

commit v3 on v2

--- a/solution.py
+++ b/solution.py
@@ -323,15 +323,25 @@
                 out[pl.ds(k * 8 + i, 32, stride=32), :] = block[k * 32 : (k + 1) * 32]
 
 
-def call(kernel, outs, scratch=()):
+def call(kernel, outs, scratch=(), kept=(), last=False):
     vmem = pl.BlockSpec(memory_space=pltpu.VMEM)
-    return lambda *args: pl.pallas_call(
-        kernel,
-        out_shape=tuple(jax.ShapeDtypeStruct(shape, F32) for shape in outs),
-        in_specs=[vmem] * len(args),
-        out_specs=(vmem,) * len(outs),
-        scratch_shapes=[pltpu.VMEM(shape, F32) for shape in scratch],
-    )(*args)
+    kind = jax.ShapeDtypeStruct if last else pltpu.VMEM
+
+    def run(*args):
+        args = [
+            pltpu.with_memory_space_constraint(a, pltpu.VMEM) if i in kept else a
+            for i, a in enumerate(args)
+        ]
+        return pl.pallas_call(
+            kernel,
+            out_shape=tuple(kind(shape, F32) for shape in outs),
+            in_specs=[vmem] * len(args),
+            out_specs=(vmem,) * len(outs),
+            scratch_shapes=[pltpu.VMEM(shape, F32) for shape in scratch],
+            compiler_params=pltpu.CompilerParams(vmem_limit_bytes=(16 if kept else 58) << 20),
+        )(*args)
+
+    return run
 
 
 def exchanged(value, axes):
@@ -367,18 +377,19 @@
         spread_kernel,
         [(8, 80, 256), (512, 256), (128, 256), (128, 128), (64, 256)],
         [(128, 128), (128, 128)],
+        kept=(0,),
     )(got, parent, gam, class_table)
     got = exchanged(sent, "z")
-    sent, r0, br = call(middle_kernel, [(8, 40, 256), (512, 256), (512, 256)])(
+    sent, r0, br = call(middle_kernel, [(8, 40, 256), (512, 256), (512, 256)], kept=range(5))(
         got, field, d_all, w1_all, own, parent, gam
     )
     got = exchanged(sent, "z")
-    (sent,) = call(fields_kernel, [(32, 104, 128)], [(512, 256), (512, 256)])(
+    (sent,) = call(fields_kernel, [(32, 104, 128)], [(512, 256), (512, 256)], kept=range(5))(
         got, r0, br, d_all, w1_all, parent, gam
     )
     got = exchanged(sent, SPLIT)
     solution_field, residual = call(
-        finish_kernel, [(1024, 128)] * 2, [(1024, 128), (1024, 128)]
+        finish_kernel, [(1024, 128)] * 2, [(1024, 128), (1024, 128)], kept=(0,), last=True
     )(got)
     return solution_field.reshape(32, 32, 128), residual.reshape(32, 32, 128)
 

time: 118 us -> 107 us (0.907)
  Pallas kernels: 19 us -> 11 us
  blocking collectives: 74.8 us -> 72.5 us
    pallas_call x5, Pallas kernels: 19 us -> 11 us  [run(): pl.pallas_call(kernel, out_shape=tuple((kind(shape, F32) for shape in out...]
    all_to_all x3, blocking collectives: 74.8 us -> 72.5 us  [exchanged(): return lax.all_to_all(value, axes, 0, 0, tiled=True)]
  transfers between devices with their start and end apart: 1 -> 1, of which waited for: 1 -> 1; matrix products, arithmetic and copies ran while one was open for 2% -> 1% of each run, Pallas kernels for 0% -> 0%
where the time goes in v3:
time: 107 us; the launch traced here: 106 us
  blocking collectives  72.5 us (68%)
  waiting for transfers between devices  12.1 us (11%)
  Pallas kernels  11 us (10%)
  starting transfers between devices  8.59 us (8%)
  other arithmetic  1.48 us (1%)
    all_to_all x3, blocking collectives, exchanged(): return lax.all_to_all(value, axes, 0, 0, tiled=True)  72.5 us
    all_to_all x1, waiting for transfers between devices, exchanged(): return lax.all_to_all(value, axes, 0, 0, tiled=True)  12.1 us
    pallas_call x5, Pallas kernels, run(): pl.pallas_call(kernel, out_shape=tuple((kind(shape, F32) for shape in out...  11 us
    all_to_all x1, starting transfers between devices, exchanged(): return lax.all_to_all(value, axes, 0, 0, tiled=True)  8.59 us
  transfers between devices with their start and end apart: 1, of which 1 were waited for; matrix products, arithmetic and copies ran while one was open for 1% of the time, Pallas kernels for 0%

profile of v3, /device:TPU:1, one launch (start us, length us, event | category | flops | bytes accessed | tf_op | source)
XLA Modules:
  0.0 106.4 jit_solution(7735432547592578780)
XLA Ops:
  0.6 0.0 copy-start
  0.6 0.0 copy-start.1
  0.7 2.5 %shard_map.113 = f32[32,48,128]{2,1,0:T(8,128)} custom-call(f32[1024,128]{1,0:T(8,128)} %bitcast.14, f32[32,32]{1,0:T(8,128)} %d.1, f32[128,128]{1,0:T(8,128)} %bitcast.15, f32[4,32]{1,0:T(4,128)} %w1.1, f32[32,128]{1,0:T(8,128)} %bitcast.16, f32[1,32]{1,0:T(1,128)} %bitcast.17, f32[4,32,128]{2,1,0:T(8,128)} %gc.1, f32[4,32]{1,0:T(4,128)} %w3.1), custom_call_target="tpu_custom_call" | custom-call | tf_op jit(solution)/shard_map/pallas_call | solution.py:335
  3.2 8.6 %all-to-all-start = ((f32[32,48,128]{2,1,0:T(8,128)}), f32[32,48,128]{2,1,0:T(8,128)S(1)}, u32[]{:S(2)}, u32[]{:S(2)}) async-start(f32[32,48,128]{2,1,0:T(8,128)} %shard_map.113), calls=%async_computation | async-start | bytes 1572864 | tf_op jit(solution)/shard_map/all_to_all | solution.py:348
  11.8 0.0 copy-done
  11.8 0.8 select_reduce_fusion.1
  12.6 0.0 copy-done.1
  12.6 0.7 select_reduce_fusion
  13.3 12.1 %all-to-all-done.got = f32[32,48,128]{2,1,0:T(8,128)S(1)} async-done(((f32[32,48,128]{2,1,0:T(8,128)}), f32[32,48,128]{2,1,0:T(8,128)S(1)}, u32[]{:S(2)}, u32[]{:S(2)}) %all-to-all-start) | async-done | bytes 786464 | tf_op jit(solution)/shard_map/all_to_all | solution.py:348
  25.4 2.2 %shard_map.114 = (f32[8,80,256]{2,1,0:T(8,128)S(1)}, f32[512,256]{1,0:T(8,128)S(1)}, f32[128,256]{1,0:T(8,128)S(1)}, f32[128,128]{1,0:T(8,128)S(1)}, f32[64,256]{1,0:T(8,128)S(1)}) custom-call(f32[32,48,128]{2,1,0:T(8,128)S(1)} %all-to-all-done.got, s32[1,256]{1,0:T(1,128)S(1)} %bitcast.8, s32[1,128]{1,0:T(1,128)S(1)} %bitcast.11, s32[32,128]{1,0:T(8,128)S(1)} %copy-done), custom_call_target="tpu_custom_call" | custom-call | tf_op jit(solution)/shard_map/pallas_call | solution.py:335
  27.7 27.0 %all_to_all.20.got = f32[8,80,256]{2,1,0:T(8,128)S(1)} all-to-all(f32[8,80,256]{2,1,0:T(8,128)S(1)} %get-tuple-element.12), channel_id=1, replica_groups=mesh['y'=4,'core'=2,'x'=4,'z'=8] {'z'}, dimensions={0} | all-to-all | bytes 1310720 | tf_op jit(solution)/shard_map/all_to_all | solution.py:348
  54.7 2.4 %shard_map.115 = (f32[8,40,256]{2,1,0:T(8,128)S(1)}, f32[512,256]{1,0:T(8,128)S(1)}, f32[512,256]{1,0:T(8,128)S(1)}) custom-call(f32[8,80,256]{2,1,0:T(8,128)S(1)} %all_to_all.20.got, f32[512,256]{1,0:T(8,128)S(1)} %get-tuple-element.13.field_in, f32[128,256]{1,0:T(8,128)S(1)} %get-tuple-element.14.d_in, f32[128,128]{1,0:T(8,128)S(1)} %get-tuple-element.15.w1_in, ...), custom_call_target="tpu_custom_call" | custom-call | tf_op jit(solution)/shard_map/pallas_call | solution.py:335
  57.1 12.3 %all_to_all.21.got = f32[8,40,256]{2,1,0:T(8,128)S(1)} all-to-all(f32[8,40,256]{2,1,0:T(8,128)S(1)} %get-tuple-element.17), channel_id=1, replica_groups=mesh['y'=4,'core'=2,'x'=4,'z'=8] {'z'}, dimensions={0} | all-to-all | bytes 655360 | tf_op jit(solution)/shard_map/all_to_all | solution.py:348
  69.4 1.7 %shard_map.116 = f32[32,104,128]{2,1,0:T(8,128)S(1)} custom-call(f32[8,40,256]{2,1,0:T(8,128)S(1)} %all_to_all.21.got, f32[512,256]{1,0:T(8,128)S(1)} %get-tuple-element.18.r0_in, f32[512,256]{1,0:T(8,128)S(1)} %get-tuple-element.19.br_in, f32[128,256]{1,0:T(8,128)S(1)} %get-tuple-element.14.d_in, f32[128,128]{1,0:T(8,128)S(1)} %get-tuple-element.15.w1_in, ...), custom_call_target="tpu_custom_call" | custom-call | tf_op jit(solution)/shard_map/pallas_call | solution.py:335
  71.1 33.2 %all_to_all.22.got = f32[32,104,128]{2,1,0:T(8,128)S(1)} all-to-all(f32[32,104,128]{2,1,0:T(8,128)S(1)} %shard_map.116), channel_id=1, replica_groups=mesh['y'=4,'core'=2,'x'=4,'z'=8] {'y','core','x'}, dimensions={0} | all-to-all | bytes 3407872 | tf_op jit(solution)/shard_map/all_to_all | solution.py:348
  104.3 2.1 %shard_map.117 = (f32[1024,128]{1,0:T(8,128)}, f32[1024,128]{1,0:T(8,128)}) custom-call(f32[32,104,128]{2,1,0:T(8,128)S(1)} %all_to_all.22.got), custom_call_target="tpu_custom_call" | custom-call | tf_op jit(solution)/shard_map/pallas_call | solution.py:335
  (2 shorter events, 0.0 us)
Async XLA Ops:
  0.6 11.2 %copy-start = (s32[32,128]{1,0:T(8,128)S(1)}, s32[32,128]{1,0:T(8,128)}, u32[]{:S(2)}) copy-start(s32[32,128]{1,0:T(8,128)} %table.1) | copy-start | bytes 49156
  0.6 11.9 %copy-start.1 = (s32[32,128]{1,0:T(8,128)S(1)}, s32[32,128]{1,0:T(8,128)}, u32[]{:S(2)}) copy-start(s32[32,128]{1,0:T(8,128)} %param.18) | copy-start | bytes 49156
  3.2 22.3 %all-to-all-start = ((f32[32,48,128]{2,1,0:T(8,128)}), f32[32,48,128]{2,1,0:T(8,128)S(1)}, u32[]{:S(2)}, u32[]{:S(2)}) async-start(f32[32,48,128]{2,1,0:T(8,128)} %shard_map.113), calls=%async_computation | async-start | bytes 1572864 | tf_op jit(solution)/shard_map/all_to_all | solution.py:348

commit v4 on v3

v4 whole, which is shorter than its diff:
```python
import jax
import jax.numpy as jnp
from jax import lax
from jax.experimental import pallas as pl
from jax.experimental.pallas import tpu as pltpu
from jax.sharding import Mesh
from jax.sharding import PartitionSpec as P

F32 = jnp.float32
BF16 = jnp.bfloat16
REG = ("y", "core")
PROD = ("x", "far", "near")
SPLIT = ("y", "core", "x", "near")
LANES = (((1,), (1,)), ((), ()))


def iota(shape, dim):
    return lax.broadcasted_iota(jnp.int32, shape, dim)


def flag(condition):
    return condition.astype(F32).astype(BF16)


def parts(value):
    high = value.astype(BF16)
    return high, (value - high.astype(F32)).astype(BF16)


def dot(a, b):
    if a.dtype == BF16:
        return sum(jnp.dot(a, p, preferred_element_type=F32) for p in parts(b))
    return sum(jnp.dot(p, b, preferred_element_type=F32) for p in parts(a))


def dot_t(value, flags):
    return sum(lax.dot_general(p, flags, LANES, preferred_element_type=F32) for p in parts(value))


def swapped(pieces):
    group = iota(pieces[0].shape, 1) // 32
    odd, upper = (group & 1) == 1, group >= 2
    a = []
    for i in (0, 2):
        a.append(jnp.where(odd, pltpu.roll(pieces[i + 1], 32, 1), pieces[i]))
        a.append(jnp.where(odd, pieces[i + 1], pltpu.roll(pieces[i], 96, 1)))
    return (
        jnp.where(upper, pltpu.roll(a[2], 64, 1), a[0]),
        jnp.where(upper, pltpu.roll(a[3], 64, 1), a[1]),
        jnp.where(upper, a[2], pltpu.roll(a[0], 64, 1)),
        jnp.where(upper, a[3], pltpu.roll(a[1], 64, 1)),
    )


def group_flags(parent):
    row = iota((128, 256), 0) % 64
    return [flag(row == parent + 32 * h) for h in range(2)]


def category_flags(places):
    row = iota((64, 256), 0)
    return [flag(row == places * 2 + h) for h in range(2)]


def grouped(field, flags):
    return dot_t(field[0], flags[0]) + dot_t(field[1], flags[1])


def ungrouped(value, flags):
    high = value.astype(BF16).astype(F32)
    both = jnp.where(iota(value.shape, 1) < 64, high, value - high).astype(BF16)
    return [jnp.dot(both, f, preferred_element_type=F32) for f in flags]


def mixed(field, precision, group_precision, flags):
    lifted = ungrouped(group_precision * grouped(field, flags), flags)
    return [precision * field[h] + lifted[h] for h in range(2)]


def categories(field, flags):
    return dot(flags[0], field[0]) + dot(flags[1], field[1])


def lifted_categories(value, places):
    both = jnp.concatenate(parts(value), axis=0)
    lane = (iota((256, 128), 1) % 64).astype(F32)
    flags = [flag(lane == places * 2.0 + h) for h in range(2)]
    return [jnp.dot(f, both, preferred_element_type=F32) for f in flags]


def steps(ref):
    return [ref[h * 256 : (h + 1) * 256, :] for h in range(2)]


def turned_square(ref):
    return jnp.concatenate([ref[:, 0:128].T, ref[:, 128:256].T], axis=0)


def pack_kernel(b, d, gi, w1, ac, w2, gc, w3, out, turned, turned_small):
    own = lax.axis_index("x") * 8 + lax.axis_index("far") * 2 + lax.axis_index("near")
    for i in range(8):
        block = jnp.concatenate(
            [b[pl.ds(k * 8 + i, 32, stride=32), :] for k in range(4)], axis=0
        )
        turned[pl.ds(i, 128, stride=8), :] = block.T
    d_turned = d[...].T
    d_rows = jnp.concatenate([d_turned[k * 8 : (k + 1) * 8] for k in range(4)], axis=1)
    w1_row = jnp.concatenate([w1[k : k + 1, :] for k in range(4)], axis=1)
    w2_row = jnp.concatenate([w2[...]] * 4, axis=1)
    gi_turned = gi[...].T
    mine = (iota((4, 32, 128), 1) == own).astype(F32)
    corner = jnp.sum(gc[...] * mine, axis=1)
    weight = jnp.sum(jnp.where(iota((4, 32), 1) == own, w3[...], 0.0), axis=1, keepdims=True)
    small = [ac[...], corner * weight, jnp.broadcast_to(weight, (4, 128))]
    small = jnp.concatenate([*small, jnp.zeros((88, 128), F32)], axis=0)
    turned_small[...] = small.T
    first, second = (turned_small[pl.ds(h, 64, stride=2), :] for h in range(2))
    corners = jnp.concatenate(
        [first[:, 32:36], second[:, 32:36], first[:, 36:40], jnp.zeros((64, 20), F32)], axis=1
    )
    last = jnp.concatenate([first[:, 0:32], second[:, 0:32], first[:, 0:32], corners], axis=1)
    lane = iota((64, 128), 1)
    last = jnp.where(lane < 96, jnp.where(lane < 64, last * w2_row, w2_row), last)
    for s in range(64):
        at = s * 28
        out[at : at + 16, :] = turned[s * 16 : (s + 1) * 16, :]
        out[at + 16 : at + 24, :] = d_rows
        out[at + 24 : at + 26, :] = gi_turned[s * 2 : (s + 1) * 2, :]
        out[at + 26 : at + 27, :] = w1_row
        out[at + 27 : at + 28, :] = last[s : s + 1, :]


def spread_kernel(
    got, parent, gam, table, out, field_out, d_out, w1_out, own_out, places_out, g_ref, k_ref
):
    for w in range(8):
        for half in range(2):
            lanes = slice(half * 128, (half + 1) * 128)
            first = [((half * 4 + g) * 8 + w) * 28 for g in range(4)]
            pieces = swapped([got[at : at + 28, :] for at in first])
            for k in range(4):
                piece = pieces[k]
                at = w * 32 + k * 8
                d_out[at : at + 8, lanes] = piece[16:24]
                for h in range(2):
                    field_out[h * 256 + at : h * 256 + at + 8, lanes] = (
                        piece[h * 8 : (h + 1) * 8] * piece[16:24]
                    )
            for h in range(2):
                own_out[w * 2 + h : w * 2 + h + 1, lanes] = pieces[h][27:28]
                own_out[16 + w * 2 + h : 17 + w * 2 + h, lanes] = pieces[2][27:28]
                own_out[32 + w * 2 + h : 33 + w * 2 + h, lanes] = pieces[3][27:28]
    for g in range(8):
        for side in range(2):
            lanes = slice(side * 128, (side + 1) * 128)
            first = [(g * 8 + side * 4 + i) * 28 + 24 for i in range(4)]
            pieces = swapped([got[at : at + 4, :] for at in first])
            for k in range(4):
                for copy in range(2):
                    for h in range(2):
                        at = copy * 64 + h * 32 + g * 4 + k
                        g_ref[at : at + 1, lanes] = pieces[k][h : h + 1] * pieces[k][2:3]
                        k_ref[at : at + 1, lanes] = pieces[k][2:3]
    w1 = turned_square(k_ref)
    w1_out[...] = w1
    places_out[...] = jnp.broadcast_to(gam[...].astype(F32), (128, 256)).T
    groups = group_flags(parent[...])
    flags = category_flags(gam[...])
    lane = iota((256, 256), 0)
    at = parent[...] // 4 * 32 + parent[...] % 4
    corner = own_out[32:48, :]
    odd = iota((16, 256), 0) % 2 == 1
    y0 = own_out[0:16, :]
    y0 += jnp.where(odd, dot(corner, flag(lane == at + 4)), dot(corner, flag(lane == at)))
    own_out[0:16, :] = y0
    d = d_out[...]
    lifted = ungrouped(turned_square(g_ref), groups)
    field = [field_out[h * 256 : (h + 1) * 256, :] + lifted[h] for h in range(2)]
    for h in range(2):
        field_out[h * 256 : (h + 1) * 256, :] = field[h]
    totals = [categories(field, flags)]
    for _ in range(2):
        field = mixed(field, d, w1, groups)
        totals.append(categories(field, flags))
    plain = flag(iota((32, 256), 0) == gam[...])
    everywhere = flag(iota((128, 256), 0) % 32 == parent[...])
    members = lax.dot_general(
        jnp.ones((8, 256), BF16), everywhere, LANES, preferred_element_type=F32
    )[0:1]
    lifted_w1 = ungrouped(w1, groups[0:1])[0]
    small = [dot(plain, v) for v in (d, d * d, d * lifted_w1)]
    row, lane = iota((128, 256), 0), iota((128, 256), 1)
    at = jnp.where(row < 32, row // 4 * 32 + row % 4, -16)
    small.append(
        dot(dot(plain, w1), flag(lane == at + 8))
        + dot(dot(plain, members * w1 * w1), flag(lane == at + 12))
    )
    count = jnp.sum((table[...] >= 0).astype(F32), axis=1, keepdims=True)
    count = jnp.where(iota((32, 1), 0) % 8 // 2 == lax.axis_index("far"), count, 0.0)
    for w in range(8):
        part = count[w // 2 * 8 : w // 2 * 8 + 8]
        part = jnp.where(iota((8, 1), 0) % 2 == w % 2, part, 0.0)
        size = jnp.sum(part, axis=0, keepdims=True)
        own_out[48 + w * 2 : 50 + w * 2, :] = jnp.broadcast_to(size, (2, 256))
    for z in range(4):
        for i in range(3):
            out[z, i * 16 : (i + 1) * 16, :] = totals[i][z * 16 : (z + 1) * 16]
        out[z, 48:64, :] = y0
        for i in range(4):
            out[z, 64 + i * 8 : 72 + i * 8, :] = small[i][z * 8 : (z + 1) * 8]


def lane_sums(value):
    rows = jnp.sum(value, axis=0, keepdims=True)
    return sum(rows[:, t * 128 : (t + 1) * 128] for t in range(value.shape[1] // 128))


def field_product(a, b):
    return lane_sums(a[0] * b[0] + a[1] * b[1])


def middle_kernel(got, field_in, d_in, w1_in, own, places_in, parent, out, r0_out, br_out):
    total = sum(got[z, 0:48, :] for z in range(4))
    small = sum(got[z, 64:96, :] for z in range(4))
    v0, v1, v2 = (total[i * 16 : (i + 1) * 16] for i in range(3))

    def repeated(first):
        rows = [
            jnp.broadcast_to(small[first + w : first + w + 1], (2, 256)) for w in range(8)
        ]
        return jnp.concatenate(rows, axis=0)

    vd, vd2, e, vw = (repeated(i * 8) for i in range(4))
    vw2 = pltpu.roll(vw, 252, 1)
    y0, w2, w3, n = (own[i * 16 : (i + 1) * 16, :] for i in range(4))
    at = parent[...] // 4 * 32 + parent[...] % 4 + 8
    places = flag(iota((256, 256), 0) == at)

    def up(value):
        return dot_t(value, places)

    def down(value):
        return dot(value, places)

    def shared(value):
        return w2 * value + down(w3 * up(value))

    sums = up(jnp.concatenate([y0, e * y0], axis=0))
    u0, ue = sums[0:16], sums[16:32]
    lifts = down(jnp.concatenate([u0, vw * u0, ue + vw2 * u0], axis=0))
    b1 = v1 + vd * y0 + lifts[16:32]
    b2 = v2 + vd2 * y0 + e * lifts[0:16] + lifts[32:48]
    g0 = v0 + n * y0
    y1 = shared(g0)
    g1 = b1 + n * y1
    y2 = shared(g1)
    k1 = vd * y1 + down(vw * up(y1))
    m1 = lane_sums(g0 * y1)
    m2 = lane_sums((2.0 * b1 + n * y1) * y1)
    m3 = lane_sums((2.0 * b2 + k1) * y1 + g1 * y2)

    groups, d, w1 = group_flags(parent[...]), d_in[...], w1_in[...]
    shares = jnp.concatenate([got[z, 48:64, :] for z in range(4)], axis=0)
    lifted = lifted_categories(shares, places_in[...])
    field = steps(field_in)
    r0 = [field[h] + lifted[h] for h in range(2)]
    br = mixed(r0, d, w1, groups)
    for h in range(2):
        r0_out[h * 256 : (h + 1) * 256, :] = r0[h]
        br_out[h * 256 : (h + 1) * 256, :] = br[h]
    rows = grouped(br, groups)
    m0 = field_product(r0, r0)
    m1 += field_product(r0, br)
    m2 += field_product(br, br)
    m3 += field_product(br, [d * v for v in br]) + 0.5 * lane_sums(w1 * rows * rows)
    moments = jnp.concatenate([m0, m1, m2, m3, jnp.zeros((4, 128), F32)], axis=0)
    moments = jnp.sum(moments, axis=1, keepdims=True)
    at_lane = iota((8, 128), 0) == iota((8, 128), 1)
    moments = jnp.sum(jnp.where(at_lane, moments, 0.0), axis=0, keepdims=True)
    for z in range(4):
        at = z * 66
        for t in range(2):
            out[at + t * 16 : at + (t + 1) * 16, :] = y1[:, t * 128 : (t + 1) * 128]
            out[at + 32 + t * 16 : at + 48 + t * 16, :] = y2[:, t * 128 : (t + 1) * 128]
        out[at + 64 : at + 66, :] = jnp.concatenate([moments] * 2, axis=0)


def fields_kernel(got, r0_in, br_in, d_in, w1_in, places_in, parent, out, f_ref, g_ref):
    groups, category = group_flags(parent[...]), places_in[...]

    def shares(first):
        tiles = [
            jnp.concatenate([got[z * 66 + at : z * 66 + at + 16, :] for z in range(4)], axis=0)
            for at in (first, first + 16)
        ]
        return jnp.concatenate(tiles, axis=1)

    first = lifted_categories(shares(0), category)
    second = lifted_categories(shares(32), category)
    br = steps(br_in)
    field = [br[h] + first[h] for h in range(2)]
    after = mixed(field, d_in[...], w1_in[...], groups)
    for h in range(2):
        f_ref[h * 256 : (h + 1) * 256, :] = field[h]
        g_ref[h * 256 : (h + 1) * 256, :] = after[h] + second[h]
    moments = sum(got[z * 66 + 64 : z * 66 + 65, :] for z in range(4))
    for w in range(8):
        for half in range(2):
            lanes = slice(half * 128, (half + 1) * 128)
            for i, ref in enumerate((r0_in, f_ref, g_ref)):
                pieces = []
                for k in range(4):
                    at = w * 32 + k * 8
                    pieces.append(
                        jnp.concatenate(
                            [ref[h * 256 + at : h * 256 + at + 8, lanes] for h in range(2)], axis=0
                        )
                    )
                pieces = swapped(pieces)
                for g in range(4):
                    at = ((half * 4 + g) * 8 + w) * 49 + i * 16
                    out[at : at + 16, :] = pieces[g]
            for g in range(4):
                at = ((half * 4 + g) * 8 + w) * 49 + 48
                out[at : at + 1, :] = moments


def finish_kernel(got, x_out, r_out, x_ref, r_ref):
    m = got[48:49, :]
    for s in range(1, 64):
        m += got[s * 49 + 48 : s * 49 + 49, :]
    m0, m1, m2, m3 = (m[:, i : i + 1] for i in range(4))
    alpha = m0 / m1
    norm = m0 - 2.0 * alpha * m1 + alpha * alpha * m2
    grown = 1.0 + norm / m0
    product = grown * grown * m1 - 2.0 * grown * alpha * m2 + alpha * alpha * m3
    later = norm / product
    on_first, on_second = alpha + later * grown, -later * alpha
    for s in range(64):
        first, second, third = (got[s * 49 + i * 16 : s * 49 + i * 16 + 16, :] for i in range(3))
        x_ref[s * 16 : (s + 1) * 16, :] = on_first * first + on_second * second
        r_ref[s * 16 : (s + 1) * 16, :] = first - on_first * second - on_second * third
    for i in range(8):
        for ref, out in ((x_ref, x_out), (r_ref, r_out)):
            block = ref[pl.ds(i, 128, stride=8), :].T
            for k in range(4):
                out[pl.ds(k * 8 + i, 32, stride=32), :] = block[k * 32 : (k + 1) * 32]


def call(kernel, outs, scratch=(), kept=(), last=False):
    vmem = pl.BlockSpec(memory_space=pltpu.VMEM)
    kind = jax.ShapeDtypeStruct if last else pltpu.VMEM

    def run(*args):
        args = [
            pltpu.with_memory_space_constraint(a, pltpu.VMEM) if i in kept else a
            for i, a in enumerate(args)
        ]
        return pl.pallas_call(
            kernel,
            out_shape=tuple(kind(shape, F32) for shape in outs),
            in_specs=[vmem] * len(args),
            out_specs=(vmem,) * len(outs),
            scratch_shapes=[pltpu.VMEM(shape, F32) for shape in scratch],
            compiler_params=pltpu.CompilerParams(vmem_limit_bytes=(16 if kept else 58) << 20),
        )(*args)

    return run


def exchanged(value, axes, blocks, tile):
    shape = value.shape
    value = value.reshape(blocks, -1, tile, shape[-1])
    return lax.all_to_all(value, axes, 0, 0, tiled=True).reshape(shape)


def row_of(table, wanted, names):
    hit = table[:, :, None] == wanted[None, None, :]
    return jnp.sum(jnp.where(hit, names[:, None, None], 0), axis=(0, 1), dtype=jnp.int32)[None]


def on_device(b, gi, ac, gc, d, w1, w2, w3, group_table, class_table):
    (sent,) = call(pack_kernel, [(64 * 28, 128)], [(1024, 128), (128, 128)])(
        b.reshape(1024, 128),
        d,
        gi.reshape(128, 128),
        w1,
        ac.reshape(32, 128),
        w2.reshape(1, 32),
        gc,
        w3,
    )
    got = exchanged(sent, SPLIT, 64, 4)
    category = jnp.arange(32, dtype=jnp.int32)
    lane = jnp.arange(256, dtype=jnp.int32)
    parent = row_of(group_table, lane, category)
    product = lane // 64 * 256 + lax.axis_index("far") * 64 + lane % 64
    place = category % 8 // 2 * 8 + category // 8 * 2 + category % 2
    gam = row_of(class_table, product, place)
    sent, field, d_all, w1_all, own, places = call(
        spread_kernel,
        [(4, 96, 256), (512, 256), (256, 256), (256, 128), (64, 256), (256, 128)],
        [(128, 256), (128, 256)],
        kept=(0,),
    )(got, parent, gam, class_table)
    got = exchanged(sent, "far", 4, 8)
    sent, r0, br = call(middle_kernel, [(4 * 66, 128), (512, 256), (512, 256)], kept=range(6))(
        got, field, d_all, w1_all, own, places, parent
    )
    got = exchanged(sent, "far", 4, 2)
    (sent,) = call(fields_kernel, [(64 * 49, 128)], [(512, 256), (512, 256)], kept=range(6))(
        got, r0, br, d_all, w1_all, places, parent
    )
    got = exchanged(sent, SPLIT, 64, 1)
    solution_field, residual = call(
        finish_kernel, [(1024, 128)] * 2, [(1024, 128), (1024, 128)], kept=(0,), last=True
    )(got)
    return solution_field.reshape(32, 32, 128), residual.reshape(32, 32, 128)


def solution(mesh):
    finer = Mesh(
        mesh.devices.reshape(4, 2, 4, 4, 2), ("y", "core", "x", "far", "near")
    )
    return jax.shard_map(
        on_device,
        mesh=finer,
        in_specs=(
            P(REG, PROD, None),
            P(REG, PROD, None),
            P(REG, PROD, None),
            P(REG, None, None),
            P(REG, PROD),
            P(REG, PROD),
            P(REG, PROD),
            P(REG, None),
            P(),
            P(),
        ),
        out_specs=(P(REG, PROD, None), P(REG, PROD, None)),
        check_vma=False,
    )
```

time: 107 us -> 101 us (0.944)
  blocking collectives: 72.5 us -> 61.2 us
  waiting for transfers between devices: 12.1 us -> 15.1 us
  starting transfers between devices: 8.59 us -> 10.3 us
  Pallas kernels: 11 us -> 12.1 us
    all_to_all x3, blocking collectives: 72.5 us -> 61.2 us  [exchanged(): return lax.all_to_all(value, axes, 0, 0, tiled=True).reshape(shape)]
    all_to_all x1, waiting for transfers between devices: 12.1 us -> 15.1 us  [exchanged(): return lax.all_to_all(value, axes, 0, 0, tiled=True).reshape(shape)]
    all_to_all x1, starting transfers between devices: 8.59 us -> 10.3 us  [exchanged(): return lax.all_to_all(value, axes, 0, 0, tiled=True).reshape(shape)]
    pallas_call x5, Pallas kernels: 11 us -> 12.1 us  [run(): pl.pallas_call(kernel, out_shape=tuple((kind(shape, F32) for shape in out...]
where the time goes in v4:
time: 101 us
  blocking collectives  61.2 us (61%)
  waiting for transfers between devices  15.1 us (15%)
  Pallas kernels  12.1 us (12%)
  starting transfers between devices  10.3 us (10%)
  other arithmetic  1.48 us (1%)
    all_to_all x3, blocking collectives, exchanged(): return lax.all_to_all(value, axes, 0, 0, tiled=True).reshape(shape)  61.2 us
    all_to_all x1, waiting for transfers between devices, exchanged(): return lax.all_to_all(value, axes, 0, 0, tiled=True).reshape(shape)  15.1 us
    pallas_call x5, Pallas kernels, run(): pl.pallas_call(kernel, out_shape=tuple((kind(shape, F32) for shape in out...  12.1 us
    all_to_all x1, starting transfers between devices, exchanged(): return lax.all_to_all(value, axes, 0, 0, tiled=True).reshape(shape)  10.3 us
  transfers between devices with their start and end apart: 1, of which 1 were waited for; matrix products, arithmetic and copies ran while one was open for 1% of the time, Pallas kernels for 0%

profile of v4, /device:TPU:1, one launch (start us, length us, event | category | flops | bytes accessed | tf_op | source)
XLA Modules:
  0.0 100.9 jit_solution(9657829366095402054)
XLA Ops:
  0.6 0.0 copy-start.1
  0.6 0.0 copy-start
  0.7 2.7 %shard_map.113 = f32[1792,128]{1,0:T(8,128)} custom-call(f32[1024,128]{1,0:T(8,128)} %bitcast.27, f32[32,32]{1,0:T(8,128)} %d.1, f32[128,128]{1,0:T(8,128)} %bitcast.28, f32[4,32]{1,0:T(4,128)} %w1.1, f32[32,128]{1,0:T(8,128)} %bitcast.29, f32[1,32]{1,0:T(1,128)} %bitcast.30, f32[4,32,128]{2,1,0:T(8,128)} %gc.1, f32[4,32]{1,0:T(4,128)} %w3.1), custom_call_target="tpu_custom_call" | custom-call | tf_op jit(solution)/shard_map/pallas_call | solution.py:359
  3.3 10.3 %all-to-all-start = ((f32[64,7,4,128]{3,2,1,0:T(4,128)}), f32[64,7,4,128]{3,2,1,0:T(4,128)S(1)}, u32[]{:S(2)}, u32[]{:S(2)}) async-start(f32[64,7,4,128]{3,2,1,0:T(4,128)} %bitcast.4), calls=%async_computation | async-start | bytes 1835008 | tf_op jit(solution)/shard_map/all_to_all | solution.py:374
  13.7 0.0 copy-done.1
  13.7 0.7 select_reduce_fusion.1
  14.5 0.0 copy-done
  14.5 0.8 select_reduce_fusion
  15.2 15.1 %all-to-all-done = f32[64,7,4,128]{3,2,1,0:T(4,128)S(1)} async-done(((f32[64,7,4,128]{3,2,1,0:T(4,128)}), f32[64,7,4,128]{3,2,1,0:T(4,128)S(1)}, u32[]{:S(2)}, u32[]{:S(2)}) %all-to-all-start) | async-done | bytes 917536 | tf_op jit(solution)/shard_map/all_to_all | solution.py:374
  30.4 2.5 %shard_map.114 = (f32[4,96,256]{2,1,0:T(8,128)S(1)}, f32[512,256]{1,0:T(8,128)S(1)}, f32[256,256]{1,0:T(8,128)S(1)}, f32[256,128]{1,0:T(8,128)S(1)}, f32[64,256]{1,0:T(8,128)S(1)}, /*index=5*/f32[256,128]{1,0:T(8,128)S(1)}) custom-call(f32[1792,128]{1,0:T(8,128)S(1)} %bitcast.18, s32[1,256]{1,0:T(1,128)S(1)} %bitcast.23, s32[1,256]{1,0:T(1,128)S(1)} %bitcast.26, ...), custom_call_target="tpu_custom_call" | custom-call | tf_op jit(solution)/shard_map/pallas_call | solution.py:359
  32.9 19.6 %all_to_all.20 = f32[4,12,8,256]{3,2,1,0:T(8,128)S(1)} all-to-all(f32[4,12,8,256]{3,2,1,0:T(8,128)S(1)} %bitcast.21), channel_id=1, replica_groups=mesh['y'=4,'core'=2,'x'=4,'far'=4,'near'=2] {'far'}, dimensions={0} | all-to-all | bytes 786432 | tf_op jit(solution)/shard_map/all_to_all | solution.py:374
  52.5 2.3 %shard_map.115 = (f32[264,128]{1,0:T(8,128)S(1)}, f32[512,256]{1,0:T(8,128)S(1)}, f32[512,256]{1,0:T(8,128)S(1)}) custom-call(f32[4,96,256]{2,1,0:T(8,128)S(1)} %bitcast.19, f32[512,256]{1,0:T(8,128)S(1)} %get-tuple-element.14.field_in, f32[256,256]{1,0:T(8,128)S(1)} %get-tuple-element.15.d_in, f32[256,128]{1,0:T(8,128)S(1)} %get-tuple-element.16.w1_in, ...), custom_call_target="tpu_custom_call" | custom-call | tf_op jit(solution)/shard_map/pallas_call | solution.py:359
  54.8 10.7 %all_to_all.21 = f32[4,33,2,128]{3,2,1,0:T(2,128)S(1)} all-to-all(f32[4,33,2,128]{3,2,1,0:T(2,128)S(1)} %bitcast.22), channel_id=1, replica_groups=mesh['y'=4,'core'=2,'x'=4,'far'=4,'near'=2] {'far'}, dimensions={0} | all-to-all | bytes 270336 | tf_op jit(solution)/shard_map/all_to_all | solution.py:374
  65.5 2.4 %shard_map.116 = f32[3136,128]{1,0:T(8,128)S(1)} custom-call(f32[264,128]{1,0:T(8,128)S(1)} %bitcast.20, f32[512,256]{1,0:T(8,128)S(1)} %get-tuple-element.20.r0_in, f32[512,256]{1,0:T(8,128)S(1)} %get-tuple-element.21.br_in, f32[256,256]{1,0:T(8,128)S(1)} %get-tuple-element.15.d_in, f32[256,128]{1,0:T(8,128)S(1)} %get-tuple-element.16.w1_in, ...), custom_call_target="tpu_custom_call" | custom-call | tf_op jit(solution)/shard_map/pallas_call | solution.py:359
  68.0 30.9 %all_to_all.22 = f32[64,49,1,128]{3,2,1,0:T(1,128)S(1)} all-to-all(f32[64,49,1,128]{3,2,1,0:T(1,128)S(1)} %bitcast.16), channel_id=1, replica_groups=mesh['y'=4,'core'=2,'x'=4,'far'=4,'near'=2] {'y','core','x','near'}, dimensions={0} | all-to-all | bytes 3211264 | tf_op jit(solution)/shard_map/all_to_all | solution.py:374
  98.8 2.1 %shard_map.117 = (f32[1024,128]{1,0:T(8,128)}, f32[1024,128]{1,0:T(8,128)}) custom-call(f32[3136,128]{1,0:T(8,128)S(1)} %bitcast.17), custom_call_target="tpu_custom_call" | custom-call | tf_op jit(solution)/shard_map/pallas_call | solution.py:359
  (2 shorter events, 0.0 us)
Async XLA Ops:
  0.6 13.1 %copy-start.1 = (s32[32,128]{1,0:T(8,128)S(1)}, s32[32,128]{1,0:T(8,128)}, u32[]{:S(2)}) copy-start(s32[32,128]{1,0:T(8,128)} %param.18) | copy-start | bytes 49156
  0.6 13.8 %copy-start = (s32[32,128]{1,0:T(8,128)S(1)}, s32[32,128]{1,0:T(8,128)}, u32[]{:S(2)}) copy-start(s32[32,128]{1,0:T(8,128)} %table.1) | copy-start | bytes 49156
  3.3 27.0 %all-to-all-start = ((f32[64,7,4,128]{3,2,1,0:T(4,128)}), f32[64,7,4,128]{3,2,1,0:T(4,128)S(1)}, u32[]{:S(2)}, u32[]{:S(2)}) async-start(f32[64,7,4,128]{3,2,1,0:T(4,128)} %bitcast.4), calls=%async_computation | async-start | bytes 1835008 | tf_op jit(solution)/shard_map/all_to_all | solution.py:374

commit v5 on v4

--- a/solution.py
+++ b/solution.py
@@ -33,10 +33,6 @@
     return sum(jnp.dot(p, b, preferred_element_type=F32) for p in parts(a))
 
 
-def dot_t(value, flags):
-    return sum(lax.dot_general(p, flags, LANES, preferred_element_type=F32) for p in parts(value))
-
-
 def swapped(pieces):
     group = iota(pieces[0].shape, 1) // 32
     odd, upper = (group & 1) == 1, group >= 2
@@ -44,12 +40,12 @@
     for i in (0, 2):
         a.append(jnp.where(odd, pltpu.roll(pieces[i + 1], 32, 1), pieces[i]))
         a.append(jnp.where(odd, pieces[i + 1], pltpu.roll(pieces[i], 96, 1)))
-    return (
-        jnp.where(upper, pltpu.roll(a[2], 64, 1), a[0]),
-        jnp.where(upper, pltpu.roll(a[3], 64, 1), a[1]),
-        jnp.where(upper, a[2], pltpu.roll(a[0], 64, 1)),
-        jnp.where(upper, a[3], pltpu.roll(a[1], 64, 1)),
-    )
+    low, high = [], []
+    for i in range(2):
+        moved = pltpu.roll(jnp.where(upper, a[i], a[i + 2]), 64, 1)
+        low.append(jnp.where(upper, moved, a[i]))
+        high.append(jnp.where(upper, a[i + 2], moved))
+    return low + high
 
 
 def group_flags(parent):
@@ -60,10 +56,6 @@
 def category_flags(places):
     row = iota((64, 256), 0)
     return [flag(row == places * 2 + h) for h in range(2)]
-
-
-def grouped(field, flags):
-    return dot_t(field[0], flags[0]) + dot_t(field[1], flags[1])
 
 
 def ungrouped(value, flags):
@@ -72,9 +64,13 @@
     return [jnp.dot(both, f, preferred_element_type=F32) for f in flags]
 
 
-def mixed(field, precision, group_precision, flags):
-    lifted = ungrouped(group_precision * grouped(field, flags), flags)
-    return [precision * field[h] + lifted[h] for h in range(2)]
+def same_parent(parent, column):
+    column = jnp.concatenate([column, column], axis=1)
+    return flag(column == parent.astype(F32))
+
+
+def mixed(field, precision, group_precision, same):
+    return [precision * v + group_precision * dot(v, same) for v in field]
 
 
 def categories(field, flags):
@@ -131,7 +127,8 @@
 
 
 def spread_kernel(
-    got, parent, gam, table, out, field_out, d_out, w1_out, own_out, places_out, g_ref, k_ref
+    got, parent, gam, table, out, field_out, d_out, w1_out, own_out, places_out, column_out,
+    g_ref, k_ref,
 ):
     for w in range(8):
         for half in range(2):
@@ -156,13 +153,17 @@
             first = [(g * 8 + side * 4 + i) * 28 + 24 for i in range(4)]
             pieces = swapped([got[at : at + 4, :] for at in first])
             for k in range(4):
-                for copy in range(2):
-                    for h in range(2):
-                        at = copy * 64 + h * 32 + g * 4 + k
-                        g_ref[at : at + 1, lanes] = pieces[k][h : h + 1] * pieces[k][2:3]
-                        k_ref[at : at + 1, lanes] = pieces[k][2:3]
+                for h in range(2):
+                    at = h * 32 + g * 4 + k
+                    g_ref[at : at + 1, lanes] = pieces[k][h : h + 1] * pieces[k][2:3]
+                k_ref[g * 4 + k : g * 4 + k + 1, lanes] = pieces[k][2:3]
+    g_ref[64:128, :] = g_ref[0:64, :]
+    for i in range(1, 4):
+        k_ref[i * 32 : (i + 1) * 32, :] = k_ref[0:32, :]
     w1 = turned_square(k_ref)
-    w1_out[...] = w1
+    column = jnp.broadcast_to(parent[...].astype(F32), (128, 256)).T
+    column_out[...] = column
+    same = same_parent(parent[...], column)
     places_out[...] = jnp.broadcast_to(gam[...].astype(F32), (128, 256)).T
     groups = group_flags(parent[...])
     flags = category_flags(gam[...])
@@ -173,22 +174,24 @@
     y0 = own_out[0:16, :]
     y0 += jnp.where(odd, dot(corner, flag(lane == at + 4)), dot(corner, flag(lane == at)))
     own_out[0:16, :] = y0
+    own_out[32:48, :] = dot(corner, flag(lane == at + 8))
     d = d_out[...]
+    w1_lifted = ungrouped(w1, groups[0:1])[0]
+    w1_out[...] = w1_lifted
     lifted = ungrouped(turned_square(g_ref), groups)
     field = [field_out[h * 256 : (h + 1) * 256, :] + lifted[h] for h in range(2)]
     for h in range(2):
         field_out[h * 256 : (h + 1) * 256, :] = field[h]
     totals = [categories(field, flags)]
     for _ in range(2):
-        field = mixed(field, d, w1, groups)
+        field = mixed(field, d, w1_lifted, same)
         totals.append(categories(field, flags))
     plain = flag(iota((32, 256), 0) == gam[...])
     everywhere = flag(iota((128, 256), 0) % 32 == parent[...])
     members = lax.dot_general(
         jnp.ones((8, 256), BF16), everywhere, LANES, preferred_element_type=F32
     )[0:1]
-    lifted_w1 = ungrouped(w1, groups[0:1])[0]
-    small = [dot(plain, v) for v in (d, d * d, d * lifted_w1)]
+    small = [dot(plain, v) for v in (d, d * d, d * w1_lifted)]
     row, lane = iota((128, 256), 0), iota((128, 256), 1)
     at = jnp.where(row < 32, row // 4 * 32 + row % 4, -16)
     small.append(
@@ -219,60 +222,50 @@
     return lane_sums(a[0] * b[0] + a[1] * b[1])
 
 
-def middle_kernel(got, field_in, d_in, w1_in, own, places_in, parent, out, r0_out, br_out):
+def middle_kernel(
+    got, field_in, d_in, w1_in, own, places_in, column, parent, out, r0_out, br_out
+):
     total = sum(got[z, 0:48, :] for z in range(4))
     small = sum(got[z, 64:96, :] for z in range(4))
     v0, v1, v2 = (total[i * 16 : (i + 1) * 16] for i in range(3))
 
-    def repeated(first):
-        rows = [
-            jnp.broadcast_to(small[first + w : first + w + 1], (2, 256)) for w in range(8)
-        ]
-        return jnp.concatenate(rows, axis=0)
-
-    vd, vd2, e, vw = (repeated(i * 8) for i in range(4))
-    vw2 = pltpu.roll(vw, 252, 1)
+    def repeated(value):
+        return jnp.concatenate(
+            [jnp.broadcast_to(value[w : w + 1], (2, 256)) for w in range(8)], axis=0
+        )
+
     y0, w2, w3, n = (own[i * 16 : (i + 1) * 16, :] for i in range(4))
-    at = parent[...] // 4 * 32 + parent[...] % 4 + 8
-    places = flag(iota((256, 256), 0) == at)
-
-    def up(value):
-        return dot_t(value, places)
-
-    def down(value):
-        return dot(value, places)
-
-    def shared(value):
-        return w2 * value + down(w3 * up(value))
-
-    sums = up(jnp.concatenate([y0, e * y0], axis=0))
-    u0, ue = sums[0:16], sums[16:32]
-    lifts = down(jnp.concatenate([u0, vw * u0, ue + vw2 * u0], axis=0))
-    b1 = v1 + vd * y0 + lifts[16:32]
-    b2 = v2 + vd2 * y0 + e * lifts[0:16] + lifts[32:48]
+    lane = iota((256, 256), 0)
+    at = parent[...] // 4 * 32 + parent[...] % 4
+    vd, vd2, e = (repeated(small[i * 8 : (i + 1) * 8]) for i in range(3))
+    vw, vw2 = (repeated(dot(small[24:32], flag(lane == at + i))) for i in (8, 12))
+    same = same_parent(parent[...], column[...])
     g0 = v0 + n * y0
-    y1 = shared(g0)
+    shared = dot(jnp.concatenate([y0, e * y0, g0], axis=0), same)
+    b1 = v1 + vd * y0 + vw * shared[0:16]
+    b2 = v2 + vd2 * y0 + (e + vw2) * shared[0:16] + shared[16:32]
+    y1 = w2 * g0 + w3 * shared[32:48]
     g1 = b1 + n * y1
-    y2 = shared(g1)
-    k1 = vd * y1 + down(vw * up(y1))
+    shared = dot(jnp.concatenate([y1, g1], axis=0), same)
+    k1 = vd * y1 + vw * shared[0:16]
+    y2 = w2 * g1 + w3 * shared[16:32]
     m1 = lane_sums(g0 * y1)
     m2 = lane_sums((2.0 * b1 + n * y1) * y1)
     m3 = lane_sums((2.0 * b2 + k1) * y1 + g1 * y2)
 
-    groups, d, w1 = group_flags(parent[...]), d_in[...], w1_in[...]
+    d, w1 = d_in[...], w1_in[...]
     shares = jnp.concatenate([got[z, 48:64, :] for z in range(4)], axis=0)
     lifted = lifted_categories(shares, places_in[...])
     field = steps(field_in)
     r0 = [field[h] + lifted[h] for h in range(2)]
-    br = mixed(r0, d, w1, groups)
+    br = mixed(r0, d, w1, same)
     for h in range(2):
         r0_out[h * 256 : (h + 1) * 256, :] = r0[h]
         br_out[h * 256 : (h + 1) * 256, :] = br[h]
-    rows = grouped(br, groups)
     m0 = field_product(r0, r0)
     m1 += field_product(r0, br)
     m2 += field_product(br, br)
-    m3 += field_product(br, [d * v for v in br]) + 0.5 * lane_sums(w1 * rows * rows)
+    m3 += field_product(br, mixed(br, d, w1, same))
     moments = jnp.concatenate([m0, m1, m2, m3, jnp.zeros((4, 128), F32)], axis=0)
     moments = jnp.sum(moments, axis=1, keepdims=True)
     at_lane = iota((8, 128), 0) == iota((8, 128), 1)
@@ -285,8 +278,8 @@
         out[at + 64 : at + 66, :] = jnp.concatenate([moments] * 2, axis=0)
 
 
-def fields_kernel(got, r0_in, br_in, d_in, w1_in, places_in, parent, out, f_ref, g_ref):
-    groups, category = group_flags(parent[...]), places_in[...]
+def fields_kernel(got, r0_in, br_in, d_in, w1_in, places_in, column, parent, out, f_ref, g_ref):
+    same, category = same_parent(parent[...], column[...]), places_in[...]
 
     def shares(first):
         tiles = [
@@ -299,7 +292,7 @@
     second = lifted_categories(shares(32), category)
     br = steps(br_in)
     field = [br[h] + first[h] for h in range(2)]
-    after = mixed(field, d_in[...], w1_in[...], groups)
+    after = mixed(field, d_in[...], w1_in[...], same)
     for h in range(2):
         f_ref[h * 256 : (h + 1) * 256, :] = field[h]
         g_ref[h * 256 : (h + 1) * 256, :] = after[h] + second[h]
@@ -325,10 +318,11 @@
                 out[at : at + 1, :] = moments
 
 
-def finish_kernel(got, x_out, r_out, x_ref, r_ref):
-    m = got[48:49, :]
-    for s in range(1, 64):
-        m += got[s * 49 + 48 : s * 49 + 49, :]
+def finish_kernel(got, x_out, r_out, x_ref, r_ref, turned, sems):
+    sums = [
+        sum(got[s * 49 + 48 : s * 49 + 49, :] for s in range(i, 64, 8)) for i in range(8)
+    ]
+    m = sum(sums)
     m0, m1, m2, m3 = (m[:, i : i + 1] for i in range(4))
     alpha = m0 / m1
     norm = m0 - 2.0 * alpha * m1 + alpha * alpha * m2
@@ -340,11 +334,19 @@
         first, second, third = (got[s * 49 + i * 16 : s * 49 + i * 16 + 16, :] for i in range(3))
         x_ref[s * 16 : (s + 1) * 16, :] = on_first * first + on_second * second
         r_ref[s * 16 : (s + 1) * 16, :] = first - on_first * second - on_second * third
-    for i in range(8):
-        for ref, out in ((x_ref, x_out), (r_ref, r_out)):
+    copies = []
+    for j, (ref, out) in enumerate(((x_ref, x_out), (r_ref, r_out))):
+        for i in range(8):
             block = ref[pl.ds(i, 128, stride=8), :].T
             for k in range(4):
-                out[pl.ds(k * 8 + i, 32, stride=32), :] = block[k * 32 : (k + 1) * 32]
+                turned[pl.ds(j * 1024 + k * 8 + i, 32, stride=32), :] = block[
+                    k * 32 : (k + 1) * 32
+                ]
+        copy = pltpu.make_async_copy(turned.at[pl.ds(j * 1024, 1024), :], out, sems.at[j])
+        copy.start()
+        copies.append(copy)
+    for copy in copies:
+        copy.wait()
 
 
 def call(kernel, outs, scratch=(), kept=(), last=False):
@@ -360,8 +362,9 @@
             kernel,
             out_shape=tuple(kind(shape, F32) for shape in outs),
             in_specs=[vmem] * len(args),
-            out_specs=(vmem,) * len(outs),
-            scratch_shapes=[pltpu.VMEM(shape, F32) for shape in scratch],
+            out_specs=(pl.BlockSpec(memory_space=pl.ANY) if last else vmem,) * len(outs),
+            scratch_shapes=[pltpu.VMEM(shape, F32) for shape in scratch]
+            + [pltpu.SemaphoreType.DMA((2,))] * last,
             compiler_params=pltpu.CompilerParams(vmem_limit_bytes=(16 if kept else 58) << 20),
         )(*args)
 
@@ -397,23 +400,27 @@
     product = lane // 64 * 256 + lax.axis_index("far") * 64 + lane % 64
     place = category % 8 // 2 * 8 + category // 8 * 2 + category % 2
     gam = row_of(class_table, product, place)
-    sent, field, d_all, w1_all, own, places = call(
+    sent, field, d_all, w1_all, own, places, column = call(
         spread_kernel,
-        [(4, 96, 256), (512, 256), (256, 256), (256, 128), (64, 256), (256, 128)],
+        [(4, 96, 256), (512, 256), (256, 256), (256, 256), (64, 256), (256, 128), (256, 128)],
         [(128, 256), (128, 256)],
         kept=(0,),
     )(got, parent, gam, class_table)
     got = exchanged(sent, "far", 4, 8)
-    sent, r0, br = call(middle_kernel, [(4 * 66, 128), (512, 256), (512, 256)], kept=range(6))(
-        got, field, d_all, w1_all, own, places, parent
+    sent, r0, br = call(middle_kernel, [(4 * 66, 128), (512, 256), (512, 256)], kept=range(7))(
+        got, field, d_all, w1_all, own, places, column, parent
     )
     got = exchanged(sent, "far", 4, 2)
-    (sent,) = call(fields_kernel, [(64 * 49, 128)], [(512, 256), (512, 256)], kept=range(6))(
-        got, r0, br, d_all, w1_all, places, parent
+    (sent,) = call(fields_kernel, [(64 * 49, 128)], [(512, 256), (512, 256)], kept=range(7))(
+        got, r0, br, d_all, w1_all, places, column, parent
     )
     got = exchanged(sent, SPLIT, 64, 1)
     solution_field, residual = call(
-        finish_kernel, [(1024, 128)] * 2, [(1024, 128), (1024, 128)], kept=(0,), last=True
+        finish_kernel,
+        [(1024, 128)] * 2,
+        [(1024, 128), (1024, 128), (2048, 128)],
+        kept=(0,),
+        last=True,
     )(got)
     return solution_field.reshape(32, 32, 128), residual.reshape(32, 32, 128)
 

time: 101 us -> 99 us (0.980)
  Pallas kernels: 12.1 us -> 9.8 us
    pallas_call x5, Pallas kernels: 12.1 us -> 9.8 us  [run(): pl.pallas_call(kernel, out_shape=tuple((kind(shape, F32) for shape in out...]
  transfers between devices with their start and end apart: 1 -> 1, of which waited for: 1 -> 1; matrix products, arithmetic and copies ran while one was open for 1% -> 2% of each run, Pallas kernels for 0% -> 0%
where the time goes in v5:
time: 99 us; the launch traced here: 98.7 us
  blocking collectives  61.2 us (62%)
  waiting for transfers between devices  15.1 us (15%)
  starting transfers between devices  10.3 us (10%)
  Pallas kernels  9.8 us (10%)
  other arithmetic  1.48 us (1%)
    all_to_all x3, blocking collectives, exchanged(): return lax.all_to_all(value, axes, 0, 0, tiled=True).reshape(shape)  61.2 us
    all_to_all x1, waiting for transfers between devices, exchanged(): return lax.all_to_all(value, axes, 0, 0, tiled=True).reshape(shape)  15.1 us
    all_to_all x1, starting transfers between devices, exchanged(): return lax.all_to_all(value, axes, 0, 0, tiled=True).reshape(shape)  10.3 us
    pallas_call x5, Pallas kernels, run(): pl.pallas_call(kernel, out_shape=tuple((kind(shape, F32) for shape in out...  9.8 us
  transfers between devices with their start and end apart: 1, of which 1 were waited for; matrix products, arithmetic and copies ran while one was open for 2% of the time, Pallas kernels for 0%

profile of v5, /device:TPU:1, one launch (start us, length us, event | category | flops | bytes accessed | tf_op | source)
XLA Modules:
  0.0 98.7 jit_solution(15459369746883945783)
XLA Ops:
  0.6 0.0 copy-start.1
  0.6 0.0 copy-start
  0.7 2.7 %shard_map.113 = f32[1792,128]{1,0:T(8,128)} custom-call(f32[1024,128]{1,0:T(8,128)} %bitcast.27, f32[32,32]{1,0:T(8,128)} %d.1, f32[128,128]{1,0:T(8,128)} %bitcast.28, f32[4,32]{1,0:T(4,128)} %w1.1, f32[32,128]{1,0:T(8,128)} %bitcast.29, f32[1,32]{1,0:T(1,128)} %bitcast.30, f32[4,32,128]{2,1,0:T(8,128)} %gc.1, f32[4,32]{1,0:T(4,128)} %w3.1), custom_call_target="tpu_custom_call" | custom-call | tf_op jit(solution)/shard_map/pallas_call | solution.py:361
  3.3 10.3 %all-to-all-start = ((f32[64,7,4,128]{3,2,1,0:T(4,128)}), f32[64,7,4,128]{3,2,1,0:T(4,128)S(1)}, u32[]{:S(2)}, u32[]{:S(2)}) async-start(f32[64,7,4,128]{3,2,1,0:T(4,128)} %bitcast.4), calls=%async_computation | async-start | bytes 1835008 | tf_op jit(solution)/shard_map/all_to_all | solution.py:377
  13.7 0.0 copy-done.1
  13.7 0.7 select_reduce_fusion.1
  14.5 0.0 copy-done
  14.5 0.8 select_reduce_fusion
  15.2 15.1 %all-to-all-done = f32[64,7,4,128]{3,2,1,0:T(4,128)S(1)} async-done(((f32[64,7,4,128]{3,2,1,0:T(4,128)}), f32[64,7,4,128]{3,2,1,0:T(4,128)S(1)}, u32[]{:S(2)}, u32[]{:S(2)}) %all-to-all-start) | async-done | bytes 917536 | tf_op jit(solution)/shard_map/all_to_all | solution.py:377
  30.4 2.2 %shard_map.114 = (f32[4,96,256]{2,1,0:T(8,128)S(1)}, f32[512,256]{1,0:T(8,128)S(1)}, f32[256,256]{1,0:T(8,128)S(1)}, f32[256,256]{1,0:T(8,128)S(1)}, f32[64,256]...) custom-call(f32[1792,128]{1,0:T(8,128)S(1)} %bitcast.18, s32[1,256]{1,0:T(1,128)S(1)} %bitcast.23, ...), custom_call_target="tpu_custom_call" | custom-call | tf_op jit(solution)/shard_map/pallas_call | solution.py:361
  32.5 19.6 %all_to_all.20 = f32[4,12,8,256]{3,2,1,0:T(8,128)S(1)} all-to-all(f32[4,12,8,256]{3,2,1,0:T(8,128)S(1)} %bitcast.21), channel_id=1, replica_groups=mesh['y'=4,'core'=2,'x'=4,'far'=4,'near'=2] {'far'}, dimensions={0} | all-to-all | bytes 786432 | tf_op jit(solution)/shard_map/all_to_all | solution.py:377
  52.2 1.2 %shard_map.115 = (f32[264,128]{1,0:T(8,128)S(1)}, f32[512,256]{1,0:T(8,128)S(1)}, f32[512,256]{1,0:T(8,128)S(1)}) custom-call(f32[4,96,256]{2,1,0:T(8,128)S(1)} %bitcast.19, f32[512,256]{1,0:T(8,128)S(1)} %get-tuple-element.15.field_in, f32[256,256]{1,0:T(8,128)S(1)} %get-tuple-element.16.d_in, f32[256,256]{1,0:T(8,128)S(1)} %get-tuple-element.17.w1_in, ...), custom_call_target="tpu_custom_call" | custom-call | tf_op jit(solution)/shard_map/pallas_call | solution.py:361
  53.4 10.7 %all_to_all.21 = f32[4,33,2,128]{3,2,1,0:T(2,128)S(1)} all-to-all(f32[4,33,2,128]{3,2,1,0:T(2,128)S(1)} %bitcast.22), channel_id=1, replica_groups=mesh['y'=4,'core'=2,'x'=4,'far'=4,'near'=2] {'far'}, dimensions={0} | all-to-all | bytes 270336 | tf_op jit(solution)/shard_map/all_to_all | solution.py:377
  64.1 1.9 %shard_map.116 = f32[3136,128]{1,0:T(8,128)S(1)} custom-call(f32[264,128]{1,0:T(8,128)S(1)} %bitcast.20, f32[512,256]{1,0:T(8,128)S(1)} %get-tuple-element.22.r0_in, f32[512,256]{1,0:T(8,128)S(1)} %get-tuple-element.23.br_in, f32[256,256]{1,0:T(8,128)S(1)} %get-tuple-element.16.d_in, f32[256,256]{1,0:T(8,128)S(1)} %get-tuple-element.17.w1_in, ...), custom_call_target="tpu_custom_call" | custom-call | tf_op jit(solution)/shard_map/pallas_call | solution.py:361
  65.9 30.9 %all_to_all.22 = f32[64,49,1,128]{3,2,1,0:T(1,128)S(1)} all-to-all(f32[64,49,1,128]{3,2,1,0:T(1,128)S(1)} %bitcast.16), channel_id=1, replica_groups=mesh['y'=4,'core'=2,'x'=4,'far'=4,'near'=2] {'y','core','x','near'}, dimensions={0} | all-to-all | bytes 3211264 | tf_op jit(solution)/shard_map/all_to_all | solution.py:377
  96.8 1.9 %shard_map.117 = (f32[1024,128]{1,0:T(8,128)}, f32[1024,128]{1,0:T(8,128)}) custom-call(f32[3136,128]{1,0:T(8,128)S(1)} %bitcast.17), custom_call_target="tpu_custom_call" | custom-call | tf_op jit(solution)/shard_map/pallas_call | solution.py:361
  (2 shorter events, 0.0 us)
Async XLA Ops:
  0.6 13.1 %copy-start.1 = (s32[32,128]{1,0:T(8,128)S(1)}, s32[32,128]{1,0:T(8,128)}, u32[]{:S(2)}) copy-start(s32[32,128]{1,0:T(8,128)} %param.18) | copy-start | bytes 49156
  0.6 13.8 %copy-start = (s32[32,128]{1,0:T(8,128)S(1)}, s32[32,128]{1,0:T(8,128)}, u32[]{:S(2)}) copy-start(s32[32,128]{1,0:T(8,128)} %table.1) | copy-start | bytes 49156
  3.3 27.0 %all-to-all-start = ((f32[64,7,4,128]{3,2,1,0:T(4,128)}), f32[64,7,4,128]{3,2,1,0:T(4,128)S(1)}, u32[]{:S(2)}, u32[]{:S(2)}) async-start(f32[64,7,4,128]{3,2,1,0:T(4,128)} %bitcast.4), calls=%async_computation | async-start | bytes 1835008 | tf_op jit(solution)/shard_map/all_to_all | solution.py:377

commit v6 on v5

--- a/solution.py
+++ b/solution.py
@@ -29,8 +29,10 @@
 
 def dot(a, b):
     if a.dtype == BF16:
-        return sum(jnp.dot(a, p, preferred_element_type=F32) for p in parts(b))
-    return sum(jnp.dot(p, b, preferred_element_type=F32) for p in parts(a))
+        a, b = jnp.concatenate([a, a], axis=1), jnp.concatenate(parts(b), axis=0)
+    else:
+        a, b = jnp.concatenate(parts(a), axis=1), jnp.concatenate([b, b], axis=0)
+    return jnp.dot(a, b, preferred_element_type=F32)
 
 
 def swapped(pieces):
@@ -278,7 +280,7 @@
         out[at + 64 : at + 66, :] = jnp.concatenate([moments] * 2, axis=0)
 
 
-def fields_kernel(got, r0_in, br_in, d_in, w1_in, places_in, column, parent, out, f_ref, g_ref):
+def fields_kernel(got, r0_in, br_in, d_in, w1_in, places_in, column, parent, out):
     same, category = same_parent(parent[...], column[...]), places_in[...]
 
     def shares(first):
@@ -293,29 +295,47 @@
     br = steps(br_in)
     field = [br[h] + first[h] for h in range(2)]
     after = mixed(field, d_in[...], w1_in[...], same)
-    for h in range(2):
-        f_ref[h * 256 : (h + 1) * 256, :] = field[h]
-        g_ref[h * 256 : (h + 1) * 256, :] = after[h] + second[h]
+    after = [after[h] + second[h] for h in range(2)]
     moments = sum(got[z * 66 + 64 : z * 66 + 65, :] for z in range(4))
-    for w in range(8):
+    rows = []
+    for one in (steps(r0_in), field, after):
         for half in range(2):
             lanes = slice(half * 128, (half + 1) * 128)
-            for i, ref in enumerate((r0_in, f_ref, g_ref)):
-                pieces = []
-                for k in range(4):
-                    at = w * 32 + k * 8
-                    pieces.append(
-                        jnp.concatenate(
-                            [ref[h * 256 + at : h * 256 + at + 8, lanes] for h in range(2)], axis=0
-                        )
-                    )
-                pieces = swapped(pieces)
-                for g in range(4):
-                    at = ((half * 4 + g) * 8 + w) * 49 + i * 16
-                    out[at : at + 16, :] = pieces[g]
+            tiles = [v.reshape(8, 4, 8, 256) for v in one]
+            k = [jnp.concatenate([t[:, i] for t in tiles], axis=0) for i in range(4)]
+            k = [v.reshape(128, 256)[:, lanes] for v in k]
+            rows += [jnp.concatenate(k[0:2], axis=1), jnp.concatenate(k[2:4], axis=1)]
+    rows = jnp.concatenate(rows, axis=0)
+    source, target = iota((256, 256), 0), iota((256, 256), 1)
+    group = source // 32
+    place = (group & 1) * 128 + ((group & 2) | (group // 4)) * 32 + source % 32
+    moves = flag(target == place)
+    high = rows.astype(BF16)
+    rest = rows - high.astype(F32)
+    rows = jnp.dot(
+        jnp.concatenate([high, *parts(rest)], axis=1),
+        jnp.concatenate([moves] * 3, axis=0),
+        preferred_element_type=F32,
+    )
+    upper = iota((128, 128), 1) >= 64
+    for i in range(3):
+        for half in range(2):
+            at = (i * 2 + half) * 256
+            pieces = [None] * 4
+            for j in range(2):
+                a, b = (rows[at + p : at + p + 128, j * 128 : (j + 1) * 128] for p in (0, 128))
+                moved = pltpu.roll(jnp.where(upper, a, b), 64, 1)
+                pieces[j] = jnp.where(upper, moved, a)
+                pieces[j + 2] = jnp.where(upper, b, moved)
             for g in range(4):
-                at = ((half * 4 + g) * 8 + w) * 49 + 48
-                out[at : at + 1, :] = moments
+                for w in range(8):
+                    to = ((half * 4 + g) * 8 + w) * 49 + i * 16
+                    for h in range(2):
+                        out[to + h * 8 : to + h * 8 + 8, :] = pieces[g][
+                            (h * 8 + w) * 8 : (h * 8 + w) * 8 + 8
+                        ]
+    for s in range(64):
+        out[s * 49 + 48 : s * 49 + 49, :] = moments
 
 
 def finish_kernel(got, x_out, r_out, x_ref, r_ref, turned, sems):
@@ -411,7 +431,7 @@
         got, field, d_all, w1_all, own, places, column, parent
     )
     got = exchanged(sent, "far", 4, 2)
-    (sent,) = call(fields_kernel, [(64 * 49, 128)], [(512, 256), (512, 256)], kept=range(7))(
+    (sent,) = call(fields_kernel, [(64 * 49, 128)], kept=range(7))(
         got, r0, br, d_all, w1_all, places, column, parent
     )
     got = exchanged(sent, SPLIT, 64, 1)

time: 99 us -> 98.3 us (level)
  no operation moved by 1% of the time
where the time goes in v6:
time: 98.3 us; the launch traced here: 98 us
  blocking collectives  61.2 us (62%)
  waiting for transfers between devices  15.1 us (15%)
  starting transfers between devices  10.3 us (10%)
  Pallas kernels  9.18 us (9%)
  other arithmetic  1.48 us (2%)
    all_to_all x3, blocking collectives, exchanged(): return lax.all_to_all(value, axes, 0, 0, tiled=True).reshape(shape)  61.2 us
    all_to_all x1, waiting for transfers between devices, exchanged(): return lax.all_to_all(value, axes, 0, 0, tiled=True).reshape(shape)  15.1 us
    all_to_all x1, starting transfers between devices, exchanged(): return lax.all_to_all(value, axes, 0, 0, tiled=True).reshape(shape)  10.3 us
    pallas_call x5, Pallas kernels, run(): pl.pallas_call(kernel, out_shape=tuple((kind(shape, F32) for shape in out...  9.18 us
  transfers between devices with their start and end apart: 1, of which 1 were waited for; matrix products, arithmetic and copies ran while one was open for 2% of the time, Pallas kernels for 0%

profile of v6, /device:TPU:1, one launch (start us, length us, event | category | flops | bytes accessed | tf_op | source)
XLA Modules:
  0.0 98.0 jit_solution(4143570929146943704)
XLA Ops:
  0.6 0.0 copy-start.1
  0.6 0.0 copy-start
  0.7 2.7 %shard_map.113 = f32[1792,128]{1,0:T(8,128)} custom-call(f32[1024,128]{1,0:T(8,128)} %bitcast.27, f32[32,32]{1,0:T(8,128)} %d.1, f32[128,128]{1,0:T(8,128)} %bitcast.28, f32[4,32]{1,0:T(4,128)} %w1.1, f32[32,128]{1,0:T(8,128)} %bitcast.29, f32[1,32]{1,0:T(1,128)} %bitcast.30, f32[4,32,128]{2,1,0:T(8,128)} %gc.1, f32[4,32]{1,0:T(4,128)} %w3.1), custom_call_target="tpu_custom_call" | custom-call | tf_op jit(solution)/shard_map/pallas_call | solution.py:381
  3.3 10.3 %all-to-all-start = ((f32[64,7,4,128]{3,2,1,0:T(4,128)}), f32[64,7,4,128]{3,2,1,0:T(4,128)S(1)}, u32[]{:S(2)}, u32[]{:S(2)}) async-start(f32[64,7,4,128]{3,2,1,0:T(4,128)} %bitcast.4), calls=%async_computation | async-start | bytes 1835008 | tf_op jit(solution)/shard_map/all_to_all | solution.py:397
  13.7 0.0 copy-done.1
  13.7 0.7 select_reduce_fusion.1
  14.5 0.0 copy-done
  14.5 0.8 select_reduce_fusion
  15.2 15.1 %all-to-all-done = f32[64,7,4,128]{3,2,1,0:T(4,128)S(1)} async-done(((f32[64,7,4,128]{3,2,1,0:T(4,128)}), f32[64,7,4,128]{3,2,1,0:T(4,128)S(1)}, u32[]{:S(2)}, u32[]{:S(2)}) %all-to-all-start) | async-done | bytes 917536 | tf_op jit(solution)/shard_map/all_to_all | solution.py:397
  30.4 2.1 %shard_map.114 = (f32[4,96,256]{2,1,0:T(8,128)S(1)}, f32[512,256]{1,0:T(8,128)S(1)}, f32[256,256]{1,0:T(8,128)S(1)}, f32[256,256]{1,0:T(8,128)S(1)}, f32[64,256]...) custom-call(f32[1792,128]{1,0:T(8,128)S(1)} %bitcast.18, s32[1,256]{1,0:T(1,128)S(1)} %bitcast.23, ...), custom_call_target="tpu_custom_call" | custom-call | tf_op jit(solution)/shard_map/pallas_call | solution.py:381
  32.5 19.6 %all_to_all.20 = f32[4,12,8,256]{3,2,1,0:T(8,128)S(1)} all-to-all(f32[4,12,8,256]{3,2,1,0:T(8,128)S(1)} %bitcast.21), channel_id=1, replica_groups=mesh['y'=4,'core'=2,'x'=4,'far'=4,'near'=2] {'far'}, dimensions={0} | all-to-all | bytes 786432 | tf_op jit(solution)/shard_map/all_to_all | solution.py:397
  52.1 1.2 %shard_map.115 = (f32[264,128]{1,0:T(8,128)S(1)}, f32[512,256]{1,0:T(8,128)S(1)}, f32[512,256]{1,0:T(8,128)S(1)}) custom-call(f32[4,96,256]{2,1,0:T(8,128)S(1)} %bitcast.19, f32[512,256]{1,0:T(8,128)S(1)} %get-tuple-element.15.field_in, f32[256,256]{1,0:T(8,128)S(1)} %get-tuple-element.16.d_in, f32[256,256]{1,0:T(8,128)S(1)} %get-tuple-element.17.w1_in, ...), custom_call_target="tpu_custom_call" | custom-call | tf_op jit(solution)/shard_map/pallas_call | solution.py:381
  53.3 10.7 %all_to_all.21 = f32[4,33,2,128]{3,2,1,0:T(2,128)S(1)} all-to-all(f32[4,33,2,128]{3,2,1,0:T(2,128)S(1)} %bitcast.22), channel_id=1, replica_groups=mesh['y'=4,'core'=2,'x'=4,'far'=4,'near'=2] {'far'}, dimensions={0} | all-to-all | bytes 270336 | tf_op jit(solution)/shard_map/all_to_all | solution.py:397
  64.0 1.3 %shard_map.116 = f32[3136,128]{1,0:T(8,128)S(1)} custom-call(f32[264,128]{1,0:T(8,128)S(1)} %bitcast.20, f32[512,256]{1,0:T(8,128)S(1)} %get-tuple-element.22.r0_in, f32[512,256]{1,0:T(8,128)S(1)} %get-tuple-element.23.br_in, f32[256,256]{1,0:T(8,128)S(1)} %get-tuple-element.16.d_in, f32[256,256]{1,0:T(8,128)S(1)} %get-tuple-element.17.w1_in, ...), custom_call_target="tpu_custom_call" | custom-call | tf_op jit(solution)/shard_map/pallas_call | solution.py:381
  65.3 30.8 %all_to_all.22 = f32[64,49,1,128]{3,2,1,0:T(1,128)S(1)} all-to-all(f32[64,49,1,128]{3,2,1,0:T(1,128)S(1)} %bitcast.16), channel_id=1, replica_groups=mesh['y'=4,'core'=2,'x'=4,'far'=4,'near'=2] {'y','core','x','near'}, dimensions={0} | all-to-all | bytes 3211264 | tf_op jit(solution)/shard_map/all_to_all | solution.py:397
  96.2 1.9 %shard_map.117 = (f32[1024,128]{1,0:T(8,128)}, f32[1024,128]{1,0:T(8,128)}) custom-call(f32[3136,128]{1,0:T(8,128)S(1)} %bitcast.17), custom_call_target="tpu_custom_call" | custom-call | tf_op jit(solution)/shard_map/pallas_call | solution.py:381
  (2 shorter events, 0.0 us)
Async XLA Ops:
  0.6 13.1 %copy-start.1 = (s32[32,128]{1,0:T(8,128)S(1)}, s32[32,128]{1,0:T(8,128)}, u32[]{:S(2)}) copy-start(s32[32,128]{1,0:T(8,128)} %param.18) | copy-start | bytes 49156
  0.6 13.8 %copy-start = (s32[32,128]{1,0:T(8,128)S(1)}, s32[32,128]{1,0:T(8,128)}, u32[]{:S(2)}) copy-start(s32[32,128]{1,0:T(8,128)} %table.1) | copy-start | bytes 49156
  3.3 27.0 %all-to-all-start = ((f32[64,7,4,128]{3,2,1,0:T(4,128)}), f32[64,7,4,128]{3,2,1,0:T(4,128)S(1)}, u32[]{:S(2)}, u32[]{:S(2)}) async-start(f32[64,7,4,128]{3,2,1,0:T(4,128)} %bitcast.4), calls=%async_computation | async-start | bytes 1835008 | tf_op jit(solution)/shard_map/all_to_all | solution.py:397

commit v7 on v6

--- a/solution.py
+++ b/solution.py
@@ -10,8 +10,12 @@
 BF16 = jnp.bfloat16
 REG = ("y", "core")
 PROD = ("x", "far", "near")
-SPLIT = ("y", "core", "x", "near")
+SPLIT = ("core", "y", "x", "near")
 LANES = (((1,), (1,)), ((), ()))
+
+
+def sender(block, w):
+    return block % 2 * 32 + block // 2 * 8 + w
 
 
 def iota(shape, dim):
@@ -135,7 +139,7 @@
     for w in range(8):
         for half in range(2):
             lanes = slice(half * 128, (half + 1) * 128)
-            first = [((half * 4 + g) * 8 + w) * 28 for g in range(4)]
+            first = [sender(half * 4 + g, w) * 28 for g in range(4)]
             pieces = swapped([got[at : at + 28, :] for at in first])
             for k in range(4):
                 piece = pieces[k]
@@ -152,7 +156,7 @@
     for g in range(8):
         for side in range(2):
             lanes = slice(side * 128, (side + 1) * 128)
-            first = [(g * 8 + side * 4 + i) * 28 + 24 for i in range(4)]
+            first = [sender(g, side * 4 + i) * 28 + 24 for i in range(4)]
             pieces = swapped([got[at : at + 4, :] for at in first])
             for k in range(4):
                 for h in range(2):
@@ -329,7 +333,7 @@
                 pieces[j + 2] = jnp.where(upper, b, moved)
             for g in range(4):
                 for w in range(8):
-                    to = ((half * 4 + g) * 8 + w) * 49 + i * 16
+                    to = sender(half * 4 + g, w) * 49 + i * 16
                     for h in range(2):
                         out[to + h * 8 : to + h * 8 + 8, :] = pieces[g][
                             (h * 8 + w) * 8 : (h * 8 + w) * 8 + 8

time: 98.3 us -> 96.6 us (0.983)
  blocking collectives: 61.2 us -> 60.2 us
where the time goes in v7:
time: 96.6 us; the launch traced here: 96.3 us
  blocking collectives  60.2 us (62%)
  waiting for transfers between devices  14.2 us (15%)
  starting transfers between devices  10.4 us (11%)
  Pallas kernels  9.18 us (10%)
  other arithmetic  1.48 us (2%)
    all_to_all x3, blocking collectives, exchanged(): return lax.all_to_all(value, axes, 0, 0, tiled=True).reshape(shape)  60.2 us
    all_to_all x1, waiting for transfers between devices, exchanged(): return lax.all_to_all(value, axes, 0, 0, tiled=True).reshape(shape)  14.2 us
    all_to_all x1, starting transfers between devices, exchanged(): return lax.all_to_all(value, axes, 0, 0, tiled=True).reshape(shape)  10.4 us
    pallas_call x5, Pallas kernels, run(): pl.pallas_call(kernel, out_shape=tuple((kind(shape, F32) for shape in out...  9.18 us
  transfers between devices with their start and end apart: 1, of which 1 were waited for; matrix products, arithmetic and copies ran while one was open for 2% of the time, Pallas kernels for 0%

profile of v7, /device:TPU:1, one launch (start us, length us, event | category | flops | bytes accessed | tf_op | source)
XLA Modules:
  0.0 96.3 jit_solution(11036351703528384956)
XLA Ops:
  0.6 0.0 copy-start.1
  0.6 0.0 copy-start
  0.7 2.7 %shard_map.113 = f32[1792,128]{1,0:T(8,128)} custom-call(f32[1024,128]{1,0:T(8,128)} %bitcast.27, f32[32,32]{1,0:T(8,128)} %d.1, f32[128,128]{1,0:T(8,128)} %bitcast.28, f32[4,32]{1,0:T(4,128)} %w1.1, f32[32,128]{1,0:T(8,128)} %bitcast.29, f32[1,32]{1,0:T(1,128)} %bitcast.30, f32[4,32,128]{2,1,0:T(8,128)} %gc.1, f32[4,32]{1,0:T(4,128)} %w3.1), custom_call_target="tpu_custom_call" | custom-call | tf_op jit(solution)/shard_map/pallas_call | solution.py:385
  3.3 10.4 %all-to-all-start = ((f32[64,7,4,128]{3,2,1,0:T(4,128)}), f32[64,7,4,128]{3,2,1,0:T(4,128)S(1)}, u32[]{:S(2)}, u32[]{:S(2)}) async-start(f32[64,7,4,128]{3,2,1,0:T(4,128)} %bitcast.4), calls=%async_computation | async-start | bytes 1835008 | tf_op jit(solution)/shard_map/all_to_all | solution.py:401
  13.8 0.0 copy-done.1
  13.8 0.7 select_reduce_fusion.1
  14.6 0.0 copy-done
  14.6 0.8 select_reduce_fusion
  15.3 14.2 %all-to-all-done = f32[64,7,4,128]{3,2,1,0:T(4,128)S(1)} async-done(((f32[64,7,4,128]{3,2,1,0:T(4,128)}), f32[64,7,4,128]{3,2,1,0:T(4,128)S(1)}, u32[]{:S(2)}, u32[]{:S(2)}) %all-to-all-start) | async-done | bytes 917536 | tf_op jit(solution)/shard_map/all_to_all | solution.py:401
  29.5 2.1 %shard_map.114 = (f32[4,96,256]{2,1,0:T(8,128)S(1)}, f32[512,256]{1,0:T(8,128)S(1)}, f32[256,256]{1,0:T(8,128)S(1)}, f32[256,256]{1,0:T(8,128)S(1)}, f32[64,256]...) custom-call(f32[1792,128]{1,0:T(8,128)S(1)} %bitcast.18, s32[1,256]{1,0:T(1,128)S(1)} %bitcast.23, ...), custom_call_target="tpu_custom_call" | custom-call | tf_op jit(solution)/shard_map/pallas_call | solution.py:385
  31.7 17.2 %all_to_all.20 = f32[4,12,8,256]{3,2,1,0:T(8,128)S(1)} all-to-all(f32[4,12,8,256]{3,2,1,0:T(8,128)S(1)} %bitcast.21), channel_id=1, replica_groups=mesh['y'=4,'core'=2,'x'=4,'far'=4,'near'=2] {'far'}, dimensions={0} | all-to-all | bytes 786432 | tf_op jit(solution)/shard_map/all_to_all | solution.py:401
  48.9 1.2 %shard_map.115 = (f32[264,128]{1,0:T(8,128)S(1)}, f32[512,256]{1,0:T(8,128)S(1)}, f32[512,256]{1,0:T(8,128)S(1)}) custom-call(f32[4,96,256]{2,1,0:T(8,128)S(1)} %bitcast.19, f32[512,256]{1,0:T(8,128)S(1)} %get-tuple-element.15.field_in, f32[256,256]{1,0:T(8,128)S(1)} %get-tuple-element.16.d_in, f32[256,256]{1,0:T(8,128)S(1)} %get-tuple-element.17.w1_in, ...), custom_call_target="tpu_custom_call" | custom-call | tf_op jit(solution)/shard_map/pallas_call | solution.py:385
  50.1 11.2 %all_to_all.21 = f32[4,33,2,128]{3,2,1,0:T(2,128)S(1)} all-to-all(f32[4,33,2,128]{3,2,1,0:T(2,128)S(1)} %bitcast.22), channel_id=1, replica_groups=mesh['y'=4,'core'=2,'x'=4,'far'=4,'near'=2] {'far'}, dimensions={0} | all-to-all | bytes 270336 | tf_op jit(solution)/shard_map/all_to_all | solution.py:401
  61.3 1.3 %shard_map.116 = f32[3136,128]{1,0:T(8,128)S(1)} custom-call(f32[264,128]{1,0:T(8,128)S(1)} %bitcast.20, f32[512,256]{1,0:T(8,128)S(1)} %get-tuple-element.22.r0_in, f32[512,256]{1,0:T(8,128)S(1)} %get-tuple-element.23.br_in, f32[256,256]{1,0:T(8,128)S(1)} %get-tuple-element.16.d_in, f32[256,256]{1,0:T(8,128)S(1)} %get-tuple-element.17.w1_in, ...), custom_call_target="tpu_custom_call" | custom-call | tf_op jit(solution)/shard_map/pallas_call | solution.py:385
  62.6 31.8 %all_to_all.22 = f32[64,49,1,128]{3,2,1,0:T(1,128)S(1)} all-to-all(f32[64,49,1,128]{3,2,1,0:T(1,128)S(1)} %bitcast.16), channel_id=1, replica_groups=mesh['y'=4,'core'=2,'x'=4,'far'=4,'near'=2] {'core','y','x','near'}, dimensions={0} | all-to-all | bytes 3211264 | tf_op jit(solution)/shard_map/all_to_all | solution.py:401
  94.4 1.9 %shard_map.117 = (f32[1024,128]{1,0:T(8,128)}, f32[1024,128]{1,0:T(8,128)}) custom-call(f32[3136,128]{1,0:T(8,128)S(1)} %bitcast.17), custom_call_target="tpu_custom_call" | custom-call | tf_op jit(solution)/shard_map/pallas_call | solution.py:385
  (2 shorter events, 0.0 us)
Async XLA Ops:
  0.6 13.2 %copy-start.1 = (s32[32,128]{1,0:T(8,128)S(1)}, s32[32,128]{1,0:T(8,128)}, u32[]{:S(2)}) copy-start(s32[32,128]{1,0:T(8,128)} %param.18) | copy-start | bytes 49156
  0.6 13.9 %copy-start = (s32[32,128]{1,0:T(8,128)S(1)}, s32[32,128]{1,0:T(8,128)}, u32[]{:S(2)}) copy-start(s32[32,128]{1,0:T(8,128)} %table.1) | copy-start | bytes 49156
  3.3 26.2 %all-to-all-start = ((f32[64,7,4,128]{3,2,1,0:T(4,128)}), f32[64,7,4,128]{3,2,1,0:T(4,128)S(1)}, u32[]{:S(2)}, u32[]{:S(2)}) async-start(f32[64,7,4,128]{3,2,1,0:T(4,128)} %bitcast.4), calls=%async_computation | async-start | bytes 1835008 | tf_op jit(solution)/shard_map/all_to_all | solution.py:401

commit v8 on v7

--- a/solution.py
+++ b/solution.py
@@ -10,12 +10,12 @@
 BF16 = jnp.bfloat16
 REG = ("y", "core")
 PROD = ("x", "far", "near")
-SPLIT = ("core", "y", "x", "near")
+SPLIT = ("core", "x", "near", "y")
 LANES = (((1,), (1,)), ((), ()))
 
 
 def sender(block, w):
-    return block % 2 * 32 + block // 2 * 8 + w
+    return block % 2 * 32 + w * 4 + block // 2
 
 
 def iota(shape, dim):

time: 96.6 us -> 96.6 us (level)
  no operation moved by 1% of the time
where the time goes in v8:
time: 96.6 us; the launch traced here: 96.3 us
  blocking collectives  60.6 us (63%)
  waiting for transfers between devices  13.8 us (14%)
  starting transfers between devices  10.4 us (11%)
  Pallas kernels  9.18 us (10%)
  other arithmetic  1.48 us (2%)
    all_to_all x3, blocking collectives, exchanged(): return lax.all_to_all(value, axes, 0, 0, tiled=True).reshape(shape)  60.6 us
    all_to_all x1, waiting for transfers between devices, exchanged(): return lax.all_to_all(value, axes, 0, 0, tiled=True).reshape(shape)  13.8 us
    all_to_all x1, starting transfers between devices, exchanged(): return lax.all_to_all(value, axes, 0, 0, tiled=True).reshape(shape)  10.4 us
    pallas_call x5, Pallas kernels, run(): pl.pallas_call(kernel, out_shape=tuple((kind(shape, F32) for shape in out...  9.18 us
  transfers between devices with their start and end apart: 1, of which 1 were waited for; matrix products, arithmetic and copies ran while one was open for 2% of the time, Pallas kernels for 0%

profile of v8, /device:TPU:1, one launch (start us, length us, event | category | flops | bytes accessed | tf_op | source)
XLA Modules:
  0.0 96.3 jit_solution(10992258291498329559)
XLA Ops:
  0.6 0.0 copy-start.1
  0.6 0.0 copy-start
  0.7 2.7 %shard_map.113 = f32[1792,128]{1,0:T(8,128)} custom-call(f32[1024,128]{1,0:T(8,128)} %bitcast.27, f32[32,32]{1,0:T(8,128)} %d.1, f32[128,128]{1,0:T(8,128)} %bitcast.28, f32[4,32]{1,0:T(4,128)} %w1.1, f32[32,128]{1,0:T(8,128)} %bitcast.29, f32[1,32]{1,0:T(1,128)} %bitcast.30, f32[4,32,128]{2,1,0:T(8,128)} %gc.1, f32[4,32]{1,0:T(4,128)} %w3.1), custom_call_target="tpu_custom_call" | custom-call | tf_op jit(solution)/shard_map/pallas_call | solution.py:385
  3.3 10.4 %all-to-all-start = ((f32[64,7,4,128]{3,2,1,0:T(4,128)}), f32[64,7,4,128]{3,2,1,0:T(4,128)S(1)}, u32[]{:S(2)}, u32[]{:S(2)}) async-start(f32[64,7,4,128]{3,2,1,0:T(4,128)} %bitcast.4), calls=%async_computation | async-start | bytes 1835008 | tf_op jit(solution)/shard_map/all_to_all | solution.py:401
  13.8 0.0 copy-done.1
  13.8 0.7 select_reduce_fusion.1
  14.6 0.0 copy-done
  14.6 0.8 select_reduce_fusion
  15.3 13.8 %all-to-all-done = f32[64,7,4,128]{3,2,1,0:T(4,128)S(1)} async-done(((f32[64,7,4,128]{3,2,1,0:T(4,128)}), f32[64,7,4,128]{3,2,1,0:T(4,128)S(1)}, u32[]{:S(2)}, u32[]{:S(2)}) %all-to-all-start) | async-done | bytes 917536 | tf_op jit(solution)/shard_map/all_to_all | solution.py:401
  29.1 2.2 %shard_map.114 = (f32[4,96,256]{2,1,0:T(8,128)S(1)}, f32[512,256]{1,0:T(8,128)S(1)}, f32[256,256]{1,0:T(8,128)S(1)}, f32[256,256]{1,0:T(8,128)S(1)}, f32[64,256]...) custom-call(f32[1792,128]{1,0:T(8,128)S(1)} %bitcast.18, s32[1,256]{1,0:T(1,128)S(1)} %bitcast.23, ...), custom_call_target="tpu_custom_call" | custom-call | tf_op jit(solution)/shard_map/pallas_call | solution.py:385
  31.3 17.4 %all_to_all.20 = f32[4,12,8,256]{3,2,1,0:T(8,128)S(1)} all-to-all(f32[4,12,8,256]{3,2,1,0:T(8,128)S(1)} %bitcast.21), channel_id=1, replica_groups=mesh['y'=4,'core'=2,'x'=4,'far'=4,'near'=2] {'far'}, dimensions={0} | all-to-all | bytes 786432 | tf_op jit(solution)/shard_map/all_to_all | solution.py:401
  48.7 1.2 %shard_map.115 = (f32[264,128]{1,0:T(8,128)S(1)}, f32[512,256]{1,0:T(8,128)S(1)}, f32[512,256]{1,0:T(8,128)S(1)}) custom-call(f32[4,96,256]{2,1,0:T(8,128)S(1)} %bitcast.19, f32[512,256]{1,0:T(8,128)S(1)} %get-tuple-element.15.field_in, f32[256,256]{1,0:T(8,128)S(1)} %get-tuple-element.16.d_in, f32[256,256]{1,0:T(8,128)S(1)} %get-tuple-element.17.w1_in, ...), custom_call_target="tpu_custom_call" | custom-call | tf_op jit(solution)/shard_map/pallas_call | solution.py:385
  49.8 11.5 %all_to_all.21 = f32[4,33,2,128]{3,2,1,0:T(2,128)S(1)} all-to-all(f32[4,33,2,128]{3,2,1,0:T(2,128)S(1)} %bitcast.22), channel_id=1, replica_groups=mesh['y'=4,'core'=2,'x'=4,'far'=4,'near'=2] {'far'}, dimensions={0} | all-to-all | bytes 270336 | tf_op jit(solution)/shard_map/all_to_all | solution.py:401
  61.3 1.3 %shard_map.116 = f32[3136,128]{1,0:T(8,128)S(1)} custom-call(f32[264,128]{1,0:T(8,128)S(1)} %bitcast.20, f32[512,256]{1,0:T(8,128)S(1)} %get-tuple-element.22.r0_in, f32[512,256]{1,0:T(8,128)S(1)} %get-tuple-element.23.br_in, f32[256,256]{1,0:T(8,128)S(1)} %get-tuple-element.16.d_in, f32[256,256]{1,0:T(8,128)S(1)} %get-tuple-element.17.w1_in, ...), custom_call_target="tpu_custom_call" | custom-call | tf_op jit(solution)/shard_map/pallas_call | solution.py:385
  62.6 31.8 %all_to_all.22 = f32[64,49,1,128]{3,2,1,0:T(1,128)S(1)} all-to-all(f32[64,49,1,128]{3,2,1,0:T(1,128)S(1)} %bitcast.16), channel_id=1, replica_groups=mesh['y'=4,'core'=2,'x'=4,'far'=4,'near'=2] {'core','x','near','y'}, dimensions={0} | all-to-all | bytes 3211264 | tf_op jit(solution)/shard_map/all_to_all | solution.py:401
  94.4 1.9 %shard_map.117 = (f32[1024,128]{1,0:T(8,128)}, f32[1024,128]{1,0:T(8,128)}) custom-call(f32[3136,128]{1,0:T(8,128)S(1)} %bitcast.17), custom_call_target="tpu_custom_call" | custom-call | tf_op jit(solution)/shard_map/pallas_call | solution.py:385
  (2 shorter events, 0.0 us)
Async XLA Ops:
  0.6 13.2 %copy-start.1 = (s32[32,128]{1,0:T(8,128)S(1)}, s32[32,128]{1,0:T(8,128)}, u32[]{:S(2)}) copy-start(s32[32,128]{1,0:T(8,128)} %param.18) | copy-start | bytes 49156
  0.6 13.9 %copy-start = (s32[32,128]{1,0:T(8,128)S(1)}, s32[32,128]{1,0:T(8,128)}, u32[]{:S(2)}) copy-start(s32[32,128]{1,0:T(8,128)} %table.1) | copy-start | bytes 49156
  3.3 25.8 %all-to-all-start = ((f32[64,7,4,128]{3,2,1,0:T(4,128)}), f32[64,7,4,128]{3,2,1,0:T(4,128)S(1)}, u32[]{:S(2)}, u32[]{:S(2)}) async-start(f32[64,7,4,128]{3,2,1,0:T(4,128)} %bitcast.4), calls=%async_computation | async-start | bytes 1835008 | tf_op jit(solution)/shard_map/all_to_all | solution.py:401
